TPU v7x, 128 devices: a whole 4x4x4 slice. The times are simulated.
128 devices in a mesh: tile: 32 (over x, z, core), cuts: 4 (over y).
Axes of the slice: x: 4, y: 4, z: 4, core: 2. Of those that a mesh axis runs over, the one named last changes fastest.
Arguments:
- amplitudes: float32 [1024, 128, 128], P(('tile', 'cuts')), may hold values from 0 to 2
- positions: int32 [1024, 2], replicated, may hold values from 0 to 3968, as said below
- probe_field: float32 [2, 128, 128], replicated, may hold values from -4 to 4
- object_slices: float32 [4, 2, 256, 4096], P('cuts', None, None, 'tile'), may hold values from -1 to 1, as said below
Outputs:
- refined_object: float32 [4, 2, 256, 4096], P('cuts', None, None, 'tile')
Inputs may be any that keep to these rules, and one draw needn't show every extreme that they name: `positions`: rows lie in 0 .. 128; every frame's 128 columns lie inside the 4096 columns. A frame's owner tile is its column // 128. Frames are read in blocks of 8 consecutive frames, one block per device of tile+cuts in mesh order; one block holds at most 2 frames of any owner tile, and some block holds exactly 2. For every cuts index, the blocks of that index hold at most 16 frames of any one owner tile, and in every draw some owner tile receives exactly 16 from them. `object_slices`: transmissions have modulus at most 1.
All inputs are finite; a program needn't handle non-finite values.
Results may differ from a plain program's by a relative error of at most 0.015.
Values may be sent and summed in bfloat16 or wider, within the bound.
A program may use at most 128 MiB of HBM per device.

v0:
```python
import math

import jax
import jax.numpy as jnp
from jax import lax
from jax.sharding import PartitionSpec as P

ITERS = 2


STEP_SIZE = 0.05
AMPLITUDE_FLOOR = 0.25


def passed_along(x, axis, by):
    peers = lax.axis_size(axis)
    pairs = [(i, i + by) for i in range(peers) if 0 <= i + by < peers]
    return lax.ppermute(x, axis, pairs)


def block_table(real_part, imag_part):
    upper = jnp.stack([real_part, imag_part], axis=1)
    lower = jnp.stack([-imag_part, real_part], axis=1)
    return jnp.stack([upper, lower], axis=0).astype(jnp.bfloat16)


def make_tables(frame_side):
    highest = lax.Precision.HIGHEST
    index = jnp.arange(frame_side, dtype=jnp.int32)
    product = index[:, None] * index[None, :] % frame_side
    angle = product.astype(jnp.float32) * (2.0 * math.pi / frame_side)
    norm_scale = 1.0 / math.sqrt(frame_side)
    four_real = jnp.cos(angle) * norm_scale
    four_imag = -jnp.sin(angle) * norm_scale
    centred = (index + frame_side // 2) % frame_side - frame_side // 2
    chirp = -math.pi * (centred * centred).astype(jnp.float32) / (4.0 * frame_side)
    chirp_real = jnp.cos(chirp)
    chirp_imag = jnp.sin(chirp)
    left_real = four_real * chirp_real[None, :] + four_imag * chirp_imag[None, :]
    left_imag = four_real * chirp_imag[None, :] - four_imag * chirp_real[None, :]
    prop_real = jnp.dot(left_real, four_real, precision=highest) - jnp.dot(
        left_imag, four_imag, precision=highest
    )
    prop_imag = jnp.dot(left_real, four_imag, precision=highest) + jnp.dot(
        left_imag, four_real, precision=highest
    )
    return (
        block_table(four_real, four_imag),
        block_table(four_real, -four_imag),
        block_table(prop_real, prop_imag),
        block_table(prop_real, -prop_imag),
    )


def right_product(field, table):
    return jnp.einsum(
        "fcij,cjdk->fdik", field.astype(jnp.bfloat16), table, preferred_element_type=jnp.float32
    )


def two_sided(field, table):
    first = right_product(field, table)
    second = right_product(jnp.swapaxes(first, -1, -2), table)
    return jnp.swapaxes(second, -1, -2)


def complex_times(left, right):
    real_part = left[..., 0, :, :] * right[..., 0, :, :] - left[..., 1, :, :] * right[..., 1, :, :]
    imag_part = left[..., 0, :, :] * right[..., 1, :, :] + left[..., 1, :, :] * right[..., 0, :, :]
    return jnp.stack([real_part, imag_part], axis=-3)


def conj_times(left, right):
    real_part = left[..., 0, :, :] * right[..., 0, :, :] + left[..., 1, :, :] * right[..., 1, :, :]
    imag_part = left[..., 0, :, :] * right[..., 1, :, :] - left[..., 1, :, :] * right[..., 0, :, :]
    return jnp.stack([real_part, imag_part], axis=-3)


def frame_patches(windows, probe_field, measured, tables):
    four, four_conj, prop, prop_conj = tables
    slice_count = windows.shape[1]
    wave = complex_times(probe_field[None], windows[:, 0].astype(jnp.float32))
    fields = []
    for level in range(1, slice_count):
        moved = two_sided(wave, prop)
        fields.append(moved)
        wave = complex_times(windows[:, level].astype(jnp.float32), moved)
    far = two_sided(wave, four)
    magnitude = jnp.sqrt(far[:, 0] * far[:, 0] + far[:, 1] * far[:, 1])
    factor = 1.0 - measured / jnp.maximum(magnitude, AMPLITUDE_FLOOR)
    back = two_sided(far * factor[:, None], four_conj)
    patches = [None] * slice_count
    for level in range(slice_count - 1, 0, -1):
        patches[level] = conj_times(fields[level - 1], back)
        back = two_sided(conj_times(windows[:, level].astype(jnp.float32), back), prop_conj)
    patches[0] = conj_times(probe_field[None], back)
    return jnp.stack(patches, axis=1)


def cut_windows(panel, frame_rows, frame_cols, frame_side):
    zero_index = jnp.zeros((), jnp.int32)

    def window_at(row_start, col_start):
        start = (zero_index, zero_index, row_start, col_start)
        return lax.dynamic_slice(
            panel, start, (panel.shape[0], panel.shape[1], frame_side, frame_side)
        )

    return jax.vmap(window_at)(frame_rows, frame_cols)


def place_patches(panel_shape, patches, frame_rows, frame_cols, weights):
    panel_height = panel_shape[-2]
    panel_width = panel_shape[-1]
    frame_side = patches.shape[-1]
    offsets = jnp.arange(frame_side, dtype=jnp.int32)
    col_target = frame_cols[:, None] + offsets[None, :]
    col_onehot = (
        col_target[:, :, None] == jnp.arange(panel_width, dtype=jnp.int32)[None, None, :]
    ).astype(jnp.bfloat16)
    row_target = frame_rows[:, None] + offsets[None, :]
    row_onehot = (
        jnp.arange(panel_height, dtype=jnp.int32)[:, None, None] == row_target[None, :, :]
    ).astype(jnp.bfloat16)
    remain = patches * weights[:, None, None, None, None]
    gathered_sum = jnp.zeros(panel_shape, jnp.float32)
    for piece_index in range(3):
        piece_part = remain.astype(jnp.bfloat16)
        remain = remain - piece_part.astype(jnp.float32)
        placed_cols = jnp.einsum(
            "fscij,fjk->fscik", piece_part, col_onehot, preferred_element_type=jnp.float32
        ).astype(jnp.bfloat16)
        gathered_sum = gathered_sum + jnp.einsum(
            "hfi,fscik->schk", row_onehot, placed_cols, preferred_element_type=jnp.float32
        )
    return gathered_sum


def reduce_gradient(term_part):
    return lax.psum_scatter(term_part, "cuts", scatter_dimension=0, tiled=True)


def add_rim(main_part, moved_rim):
    extra = main_part.shape[-1] - moved_rim.shape[-1]
    return main_part + moved_rim


def body(amplitudes, positions, probe_field, object_slices):
    tile_count = lax.axis_size("tile")
    cut_count = lax.axis_size("cuts")
    tile_id = lax.axis_index("tile")
    cut_id = lax.axis_index("cuts")
    frame_side = probe_field.shape[-1]
    frames_held = amplitudes.shape[0]
    tile_width = object_slices.shape[-1]
    total_frames = positions.shape[0]
    reader_count = total_frames // frames_held
    capacity = max(2, 2 * frames_held // tile_count)
    max_load = 2 * frames_held
    row_list = positions[:, 0]
    col_list = positions[:, 1]
    owner = col_list // tile_width
    owner_grid = owner.reshape(reader_count, frames_held)
    earlier = jnp.tril(jnp.ones((frames_held, frames_held), jnp.int32), -1)
    same_owner = (owner_grid[:, :, None] == owner_grid[:, None, :]).astype(jnp.int32)
    slot_grid = jnp.sum(same_owner * earlier[None], axis=2)
    slot_list = slot_grid.reshape(total_frames)
    reader_self = tile_id * cut_count + cut_id
    my_owner = lax.dynamic_index_in_dim(owner_grid, reader_self, 0, keepdims=False)
    my_slot = lax.dynamic_index_in_dim(slot_grid, reader_self, 0, keepdims=False)
    target = my_owner * capacity + my_slot
    source = (
        jnp.full((tile_count * capacity,), frames_held, jnp.int32)
        .at[target]
        .set(jnp.arange(frames_held, dtype=jnp.int32))
    )
    padded = jnp.concatenate(
        [amplitudes, jnp.zeros((1, frame_side, frame_side), amplitudes.dtype)], axis=0
    )
    outgoing = jnp.take(padded, source, axis=0).reshape(
        tile_count, capacity, frame_side, frame_side
    )
    incoming = lax.all_to_all(outgoing, "tile", split_axis=0, concat_axis=0, tiled=True)
    reader_of = jnp.arange(total_frames, dtype=jnp.int32) // frames_held
    mine = (owner == tile_id) & (reader_of % cut_count == cut_id)
    rank_list = jnp.cumsum(mine.astype(jnp.int32)) - 1
    spot_list = jnp.where(mine, rank_list, max_load)
    chosen = (
        jnp.zeros((max_load,), jnp.int32)
        .at[spot_list]
        .set(jnp.arange(total_frames, dtype=jnp.int32), mode="drop")
    )
    live_weight = jnp.zeros((max_load,), jnp.float32).at[spot_list].set(1.0, mode="drop")
    flat_slot = reader_of // cut_count * capacity + slot_list
    picked = jnp.take(flat_slot, chosen)
    frames_in = jnp.take(
        incoming.reshape(tile_count * capacity, frame_side, frame_side), picked, axis=0
    )
    frame_rows = jnp.take(row_list, chosen)
    frame_cols = jnp.take(col_list, chosen) - tile_id * tile_width
    tables = make_tables(frame_side)
    current = object_slices
    for turn in range(ITERS):
        stacked = lax.all_gather(current.astype(jnp.bfloat16), "cuts", axis=0, tiled=True)
        next_rim = passed_along(stacked, "tile", -1)
        panel = jnp.concatenate([stacked, next_rim], axis=-1)
        windows = cut_windows(panel, frame_rows, frame_cols, frame_side)
        patches = frame_patches(windows, probe_field, frames_in, tables)
        term = place_patches(panel.shape, patches, frame_rows, frame_cols, live_weight)
        moved = passed_along(term[..., tile_width:], "tile", 1)
        share = reduce_gradient(add_rim(term[..., :tile_width], moved))
        current = current - STEP_SIZE * share
    return current


def solution(mesh):
    in_specs = (P(("tile", "cuts"), None, None), P(), P(), P("cuts", None, None, "tile"))
    out_specs = P("cuts", None, None, "tile")
    return jax.shard_map(body, mesh=mesh, in_specs=in_specs, out_specs=out_specs, check_vma=False)
```

profile of v0, /device:TPU:0, one launch (start us, length us, event | category | flops | bytes accessed | tf_op | source)
XLA Modules:
  0.0 458.6 jit_solution(10593045391714817191)
XLA Ops:
  7.5 13.4 %all_gather.6 = bf16[4,2,256,128]{3,2,1,0:T(8,128)(2,1)S(1)} all-gather(bf16[1,2,256,128]{3,2,1,0:T(8,128)(2,1)S(1)} %convert_element_type.304), channel_id=1, replica_groups=mesh['tile'=32,'cuts'=4] {'cuts'}, dimensions={0}, use_global_device_ids=true | all-gather | bytes 655360 | tf_op jit(solution)/shard_map/all_gather | solution.py:204
  29.6 4.5 broadcast_select_fusion
  34.1 9.0 %all-to-all-start = ((f32[32,2,128,128]{3,2,1,0:T(8,128)}), f32[32,2,128,128]{3,2,1,0:T(8,128)}, u32[]{:S(2)}, u32[]{:S(2)}) async-start(f32[32,2,128,128]{3,2,1,0:T(8,128)} %broadcast_select_fusion), calls=%async_computation | async-start | bytes 8388608 | tf_op jit(solution)/shard_map/all_to_all | solution.py:183
  44.9 4.3 scatter_custom_fusion
  52.8 4.8 %scatter_custom_fusion.2 = f32[16]{0:T(128)} fusion(s32[1024]{0:T(1024)S(1)} %bitcast.768, f32[1024]{0:T(1024)S(1)} %broadcast.687, f32[]{:T(128)} %constant.180.clone.1), kind=kCustom, calls=%fused_computation.444 | custom fusion | bytes 68 | tf_op jit(solution)/shard_map/scatter | solution.py:193
  62.3 44.7 %while.2 = (s32[]{:T(128)}, bf16[4,2,256,256]{3,2,1,0:T(8,128)(2,1)S(1)}, s32[16,4]{0,1:T(4,128)S(1)}, bf16[16,4,2,128,128]{4,3,2,0,1:T(8,128)(2,1)}, s32[]{:T(128)}) while((s32[]{:T(128)}, bf16[4,2,256,256]{3,2,1,0:T(8,128)(2,1)S(1)}, s32[16,4]{0,1:T(4,128)S(1)}, bf16[16,4,2,128,128]{4,3,2,0,1:T(8,128)(2,1)}, s32[]{:T(128)}) %tuple.101), condition=%wide.while_cond, body=%wide.while_body.sunk | while | flops 2 | bytes 525937 | solution.py:105
  107.1 5.1 %bitcast_convert_fusion.20 = (f32[16,2,128,128]{3,2,1,0:T(8,128)}, f32[16,2,128,128]{3,2,1,0:T(8,128)}, f32[16,2,128,128]{3,2,1,0:T(8,128)}, f32[16,2,128,128]{3,2,1,0:T(8,128)S(1)}) fusion(bf16[16,4,2,128,128]{4,3,2,0,1:T(8,128)(2,1)} %get-tuple-element.13), kind=kLoop, calls=%fused_computation.200 | loop fusion | flops 2097152 | bytes 12582912 | tf_op jit(solution)/shard_map/convert_element_type | solution.py:95
  133.5 4.1 convolution_bitcast_fusion.14
  137.7 5.4 %add_convert_fusion.9 = (bf16[16,1,128,128]{3,2,1,0:T(8,128)(2,1)}, bf16[16,1,128,128]{3,2,1,0:T(8,128)(2,1)}, f32[16,1,128,128]{3,2,1,0:T(8,128)}, f32[16,1,128,128]{3,2,1,0:T(8,128)}) fusion(f32[16,2,128,128]{3,2,1,0:T(8,128)} %convolution_bitcast_fusion.14, f32[16,2,128,128]{3,2,1,0:T(8,128)} %get-tuple-element.99, ...), kind=kLoop, calls=%fused_computation.251 | loop fusion | flops 3670016 | bytes 9437184 | tf_op jit(solution)/shard_map/convert.26
  143.1 3.3 convolution_bitcast_fusion.8
  146.4 5.4 %add_convert_fusion.8 = (bf16[16,1,128,128]{3,2,1,0:T(8,128)(2,1)}, bf16[16,1,128,128]{3,2,1,0:T(8,128)(2,1)}, f32[16,1,128,128]{3,2,1,0:T(8,128)}, f32[16,1,128,128]{3,2,1,0:T(8,128)}) fusion(f32[16,2,128,128]{3,2,1,0:T(8,128)} %convolution_bitcast_fusion.8, f32[16,2,128,128]{3,2,1,0:T(8,128)} %get-tuple-element.100, ...), kind=kLoop, calls=%fused_computation.249 | loop fusion | flops 3670016 | bytes 9437184 | tf_op jit(solution)/shard_map/convert.24
  155.2 4.7 %add_convert_fusion.7 = (bf16[16,1,128,128]{3,2,1,0:T(8,128)(2,1)}, bf16[16,1,128,128]{3,2,1,0:T(8,128)(2,1)}, f32[16,1,128,128]{3,2,1,0:T(8,128)}, f32[16,1,128,128]{3,2,1,0:T(8,128)}) fusion(f32[16,2,128,128]{3,2,1,0:T(8,128)} %convolution_bitcast_fusion.7, f32[16,2,128,128]{3,2,1,0:T(8,128)} %get-tuple-element.101, ...), kind=kLoop, calls=%fused_computation.247 | loop fusion | flops 3670016 | bytes 9437184 | tf_op jit(solution)/shard_map/convert.22
  167.4 6.4 %fusion.359 = (bf16[16,4,2,128,128]{4,3,2,0,1:T(8,128)(2,1)}, bf16[16,4,2,128,128]{4,3,2,0,1:T(8,128)(2,1)}, bf16[16,4,2,128,128]{4,3,2,0,1:T(8,128)(2,1)}) fusion(f32[16]{0:T(128)S(1)} %copy-done.22, f32[16,1,2,128,128]{4,3,2,0,1:T(8,128)S(1)} %maximum_bitcast_fusion.3, f32[16,1,2,128,128]{4,3,2,0,1:T(8,128)S(1)} %maximum_bitcast_fusion.2, ...), kind=kLoop, calls=%fused_computation.482 | loop fusion | flops 23068672 | bytes 20971584 | tf_op jit(solution)/shard_map/convert_element_type | solution.py:128
  173.8 8.1 %fusion.8 = f32[4,2,256,256,1]{3,2,4,1,0:T(8,128)} fusion(bf16[16,4,2,128,128]{4,3,2,0,1:T(8,128)(2,1)} %get-tuple-element.61, s32[16,128]{1,0:T(8,128)S(1)} %get-tuple-element.150, s32[16,128]{1,0:T(8,128)S(1)} %copy-done.19), kind=kOutput, calls=%fused_computation.25 | convolution fusion | flops 3226468352 | bytes 6307840 | tf_op jit(solution)/shard_map/hfi,fscik->schk/dot_general | solution.py:133
  181.9 8.2 %fusion.6 = f32[4,2,256,256,1]{3,2,4,1,0:T(8,128)} fusion(bf16[16,4,2,128,128]{4,3,2,0,1:T(8,128)(2,1)} %get-tuple-element.62, s32[16,128]{1,0:T(8,128)S(1)} %get-tuple-element.150, s32[16,128]{1,0:T(8,128)S(1)} %copy-done.19), kind=kOutput, calls=%fused_computation.22 | convolution fusion | flops 3226468352 | bytes 6307840 | tf_op jit(solution)/shard_map/hfi,fscik->schk/dot_general | solution.py:133
  190.1 8.3 %fusion.39 = f32[4,2,256,256]{2,3,1,0:T(8,128)S(1)} fusion(f32[4,2,256,256,1]{3,2,4,1,0:T(8,128)} %fusion.6, f32[4,2,256,256,1]{3,2,4,1,0:T(8,128)} %fusion.8, bf16[16,4,2,128,128]{4,3,2,0,1:T(8,128)(2,1)} %get-tuple-element.60, s32[16,128]{1,0:T(8,128)S(1)} %get-tuple-element.150, s32[16,128]{1,0:T(8,128)} %get-tuple-element.151), kind=kOutput, calls=%fused_computation.70 | convolution fusion | flops 3227516928 | bytes 10502144 | tf_op jit(solution)/shard_map/hfi,fscik->schk/dot_general | solution.py:133
  205.3 36.0 %reduce-scatter.3.cloned.1.call-done = f32[1,2,256,128]{2,3,1,0:T(8,128)} async-done(((f32[4,2,256,128]{2,3,1,0:T(8,128)}), f32[1,2,256,128]{2,3,1,0:T(8,128)}) %reduce-scatter.3.cloned.1.call-update) | async-done | bytes 262160 | tf_op jit(solution)/shard_map/reduce_scatter | solution.py:140
  242.4 12.8 %all_gather.7 = bf16[4,2,256,128]{3,2,1,0:T(8,128)(2,1)S(1)} all-gather(bf16[1,2,256,128]{3,2,1,0:T(8,128)(2,1)S(1)} %copy.237), channel_id=1, replica_groups=mesh['tile'=32,'cuts'=4] {'cuts'}, dimensions={0}, use_global_device_ids=true | all-gather | bytes 655360 | tf_op jit(solution)/shard_map/all_gather | solution.py:204
  262.1 46.3 %while.3 = (s32[]{:T(128)}, bf16[4,2,256,256]{3,2,1,0:T(8,128)(2,1)S(1)}, s32[16,4]{0,1:T(4,128)S(1)}, bf16[16,4,2,128,128]{4,3,2,0,1:T(8,128)(2,1)}, s32[]{:T(128)}) while((s32[]{:T(128)}, bf16[4,2,256,256]{3,2,1,0:T(8,128)(2,1)S(1)}, s32[16,4]{0,1:T(4,128)S(1)}, bf16[16,4,2,128,128]{4,3,2,0,1:T(8,128)(2,1)}, s32[]{:T(128)}) %tuple.111), condition=%wide.while_cond.1, body=%wide.while_body.1.sunk | while | flops 2 | bytes 525937 | solution.py:105
  308.4 5.2 %bitcast_convert_fusion.16 = (f32[16,2,128,128]{3,2,1,0:T(8,128)}, f32[16,2,128,128]{3,2,1,0:T(8,128)}, f32[16,2,128,128]{3,2,1,0:T(8,128)}, f32[16,2,128,128]{3,2,1,0:T(8,128)S(1)}) fusion(bf16[16,4,2,128,128]{4,3,2,0,1:T(8,128)(2,1)} %get-tuple-element.21), kind=kLoop, calls=%fused_computation.194 | loop fusion | flops 2097152 | bytes 12582912 | tf_op jit(solution)/shard_map/convert_element_type | solution.py:95
  323.0 3.5 subtract_convert_fusion.6
  329.9 3.6 subtract_convert_fusion.5
  339.9 3.9 convolution_bitcast_fusion.12
  343.8 5.0 %add_convert_fusion.2 = (bf16[16,1,128,128]{3,2,1,0:T(8,128)(2,1)}, bf16[16,1,128,128]{3,2,1,0:T(8,128)(2,1)}, f32[16,1,128,128]{3,2,1,0:T(8,128)S(1)}, f32[16,1,128,128]{3,2,1,0:T(8,128)}) fusion(f32[16,2,128,128]{3,2,1,0:T(8,128)} %convolution_bitcast_fusion.12, f32[16,2,128,128]{3,2,1,0:T(8,128)} %get-tuple-element.77, ...), kind=kLoop, calls=%fused_computation.217 | loop fusion | flops 3670016 | bytes 9437184 | tf_op jit(solution)/shard_map/convert.12
  352.1 5.4 %add_convert_fusion.1 = (bf16[16,1,128,128]{3,2,1,0:T(8,128)(2,1)}, bf16[16,1,128,128]{3,2,1,0:T(8,128)(2,1)}, f32[16,1,128,128]{3,2,1,0:T(8,128)}, f32[16,1,128,128]{3,2,1,0:T(8,128)}) fusion(f32[16,2,128,128]{3,2,1,0:T(8,128)} %convolution_bitcast_fusion.2, f32[16,2,128,128]{3,2,1,0:T(8,128)} %get-tuple-element.78, ...), kind=kLoop, calls=%fused_computation.215 | loop fusion | flops 3670016 | bytes 9437184 | tf_op jit(solution)/shard_map/convert.10
  360.8 4.6 %add_convert_fusion = (bf16[16,1,128,128]{3,2,1,0:T(8,128)(2,1)}, bf16[16,1,128,128]{3,2,1,0:T(8,128)(2,1)}, f32[16,1,128,128]{3,2,1,0:T(8,128)}, f32[16,1,128,128]{3,2,1,0:T(8,128)}) fusion(f32[16,2,128,128]{3,2,1,0:T(8,128)} %convolution_bitcast_fusion.1, f32[16,2,128,128]{3,2,1,0:T(8,128)} %get-tuple-element.79, ...), kind=kLoop, calls=%fused_computation.213 | loop fusion | flops 3670016 | bytes 9437184 | tf_op jit(solution)/shard_map/convert.8
  372.2 6.4 %fusion.358 = (bf16[16,4,2,128,128]{4,3,2,0,1:T(8,128)(2,1)}, bf16[16,4,2,128,128]{4,3,2,0,1:T(8,128)(2,1)}, bf16[16,4,2,128,128]{4,3,2,0,1:T(8,128)(2,1)}) fusion(f32[16]{0:T(128)S(1)} %copy-done.22, f32[16,1,2,128,128]{4,3,2,0,1:T(8,128)S(1)} %maximum_bitcast_fusion.7, f32[16,1,2,128,128]{4,3,2,0,1:T(8,128)S(1)} %maximum_bitcast_fusion.6, ...), kind=kLoop, calls=%fused_computation.481 | loop fusion | flops 23068672 | bytes 20971584 | tf_op jit(solution)/shard_map/convert_element_type | solution.py:128
  378.6 8.1 %fusion.2 = f32[4,2,256,256,1]{3,2,4,1,0:T(8,128)} fusion(bf16[16,4,2,128,128]{4,3,2,0,1:T(8,128)(2,1)} %get-tuple-element.58, s32[16,128]{1,0:T(8,128)S(1)} %get-tuple-element.150, s32[16,128]{1,0:T(8,128)S(1)} %copy-done.20), kind=kOutput, calls=%fused_computation.17 | convolution fusion | flops 3226468352 | bytes 6307840 | tf_op jit(solution)/shard_map/hfi,fscik->schk/dot_general | solution.py:133
  386.8 8.2 %fusion = f32[4,2,256,256,1]{3,2,4,1,0:T(8,128)} fusion(bf16[16,4,2,128,128]{4,3,2,0,1:T(8,128)(2,1)} %get-tuple-element.59, s32[16,128]{1,0:T(8,128)S(1)} %get-tuple-element.150, s32[16,128]{1,0:T(8,128)S(1)} %copy-done.20), kind=kOutput, calls=%fused_computation.14 | convolution fusion | flops 3226468352 | bytes 6307840 | tf_op jit(solution)/shard_map/hfi,fscik->schk/dot_general | solution.py:133
  395.0 8.4 %fusion.38 = f32[4,2,256,256]{2,3,1,0:T(8,128)S(1)} fusion(f32[4,2,256,256,1]{3,2,4,1,0:T(8,128)} %fusion, f32[4,2,256,256,1]{3,2,4,1,0:T(8,128)} %fusion.2, bf16[16,4,2,128,128]{4,3,2,0,1:T(8,128)(2,1)} %get-tuple-element.57, s32[16,128]{1,0:T(8,128)S(1)} %get-tuple-element.150, s32[16,128]{1,0:T(8,128)S(1)} %copy-done.20), kind=kOutput, calls=%fused_computation.65 | convolution fusion | flops 3227516928 | bytes 10502144 | tf_op jit(solution)/shard_map/hfi,fscik->schk/dot_general | solution.py:133
  403.5 8.7 %collective-permute-start.3 = (f32[4,2,256,128]{2,3,1,0:T(8,128)S(1)}, f32[4,2,256,128]{2,3,1,0:T(8,128)S(1)}, u32[]{:S(2)}, u32[]{:S(2)}) collective-permute-start(f32[4,2,256,128]{2,3,1,0:T(8,128)S(1)} %slice.507), channel_id=1, source_target_pairs={{0,4},{4,8},{8,12},{12,16},{16,20},{20,24},{24,28},{28,32},{32,36}... | collective-permute-start | bytes 3145736 | tf_op jit(solution)/shard_map/ppermute | solution.py:18
  415.6 33.9 %reduce-scatter.5.cloned.1.call-done = f32[1,2,256,128]{2,3,1,0:T(8,128)} async-done(((f32[4,2,256,128]{2,3,1,0:T(8,128)}), f32[1,2,256,128]{2,3,1,0:T(8,128)}) %reduce-scatter.5.cloned.1.call-update) | async-done | bytes 262160 | tf_op jit(solution)/shard_map/reduce_scatter | solution.py:140
  (251 shorter events, 195.0 us)
Async XLA Ops:
  20.9 38.2 %collective-permute-start = (bf16[4,2,256,128]{3,2,1,0:T(8,128)(2,1)S(1)}, bf16[4,2,256,128]{3,2,1,0:T(8,128)(2,1)S(1)}, u32[]{:S(2)}, u32[]{:S(2)}) collective-permute-start(bf16[4,2,256,128]{3,2,1,0:T(8,128)(2,1)S(1)} %all_gather.6), channel_id=1, source_target_pairs={{4,0},{8,4},{12,8},{16,12},{20,16},{24,20},{28,24},{32,28},{36,32}... | collective-permute-start | bytes 1572872 | tf_op jit(solution)/shard_map/ppermute | solution.py:18
  34.1 93.5 %all-to-all-start = ((f32[32,2,128,128]{3,2,1,0:T(8,128)}), f32[32,2,128,128]{3,2,1,0:T(8,128)}, u32[]{:S(2)}, u32[]{:S(2)}) async-start(f32[32,2,128,128]{3,2,1,0:T(8,128)} %broadcast_select_fusion), calls=%async_computation | async-start | bytes 8388608 | tf_op jit(solution)/shard_map/all_to_all | solution.py:183
  43.1 198.1 %reduce-scatter.3.cloned.1.call-start = ((), (), s32[]{:S(2)}) async-start(), calls=%async_computation.3 | async-start | bytes 1310720 | tf_op jit(solution)/shard_map/reduce_scatter | solution.py:140
  43.8 15.3 %copy-start.18 = (f32[2,128,128]{2,1,0:T(8,128)S(1)}, f32[2,128,128]{2,1,0:T(8,128)}, u32[]{:S(2)}) copy-start(f32[2,128,128]{2,1,0:T(8,128)} %param.8) | copy-start | bytes 393220
  162.1 1.2 copy-start.9
  162.1 1.5 copy-start.10
  163.6 1.2 copy-start.5
  163.6 1.5 copy-start.6
  165.2 1.2 copy-start.1
  165.2 1.5 copy-start.2
  166.7 0.7 copy-start.22
  167.4 6.4 %copy-start.19 = (s32[16,128]{1,0:T(8,128)S(1)}, s32[16,128]{1,0:T(8,128)}, u32[]{:S(2)}) copy-start(s32[16,128]{1,0:T(8,128)} %get-tuple-element.151) | copy-start | bytes 24580
  198.6 4.4 collective-permute-start.1
  204.1 245.3 %reduce-scatter.5.cloned.1.call-start = ((), (), s32[]{:S(2)}) async-start(), calls=%async_computation.4 | async-start | bytes 1310720 | tf_op jit(solution)/shard_map/reduce_scatter | solution.py:140
  205.3 51.2 %copy-start.11 = (f32[1,2,256,128]{2,3,1,0:T(8,128)}, f32[1,2,256,128]{2,3,1,0:T(8,128)S(1)}, u32[]{:S(2)}) copy-start(f32[1,2,256,128]{2,3,1,0:T(8,128)S(1)} %copy.236) | copy-start | bytes 786436
  255.2 3.8 collective-permute-start.2
  329.9 3.6 copy-start.15
  329.9 3.6 copy-start.16
  333.4 3.3 copy-start.21
  336.8 3.1 copy-start.13
  336.8 3.1 copy-start.14
  367.7 1.2 copy-start.7
  367.7 1.5 copy-start.8
  369.2 1.2 copy-start.3
  369.2 1.5 copy-start.4
  370.8 1.2 copy-start
  372.2 6.4 %copy-start.20 = (s32[16,128]{1,0:T(8,128)S(1)}, s32[16,128]{1,0:T(8,128)}, u32[]{:S(2)}) copy-start(s32[16,128]{1,0:T(8,128)} %get-tuple-element.151) | copy-start | bytes 24580
  403.5 46.0 %copy-start.12 = (f32[1,2,256,128]{2,3,1,0:T(8,128)S(1)}, f32[1,2,256,128]{2,3,1,0:T(8,128)}, u32[]{:S(2)}) copy-start(f32[1,2,256,128]{2,3,1,0:T(8,128)} %copy-done.11) | copy-start | bytes 786436
  403.5 46.0 %copy-start.17 = (f32[1,2,256,128]{2,3,1,0:T(8,128)S(1)}, f32[1,2,256,128]{2,3,1,0:T(8,128)}, u32[]{:S(2)}) copy-start(f32[1,2,256,128]{2,3,1,0:T(8,128)} %reduce-scatter.3.cloned.1.call-done) | copy-start | bytes 786436
  403.5 10.9 %collective-permute-start.3 = (f32[4,2,256,128]{2,3,1,0:T(8,128)S(1)}, f32[4,2,256,128]{2,3,1,0:T(8,128)S(1)}, u32[]{:S(2)}, u32[]{:S(2)}) collective-permute-start(f32[4,2,256,128]{2,3,1,0:T(8,128)S(1)} %slice.507), channel_id=1, source_target_pairs={{0,4},{4,8},{8,12},{12,16},{16,20},{20,24},{24,28},{28,32},{32,36}... | collective-permute-start | bytes 3145736 | tf_op jit(solution)/shard_map/ppermute | solution.py:18
Sparse Core Ops, SparseCore 0:
  204.3 36.9 reduce-scatter.2
  415.7 33.6 reduce-scatter.4
where the time goes:
time: 466 us; the launch traced here: 459 us
  local copies, waits for them, and re-layouts  127 us (27%)
  matrix products  96.5 us (21%)
  other arithmetic  95.2 us (20%)
  waiting for transfers between devices  76.8 us (16%)
  blocking collectives  26.2 us (6%)
  starting transfers between devices  22.6 us (5%)
  between operations  14.4 us (3%)
    gather x96, local copies, waits for them, and re-layouts  90.8 us
    reduce_scatter x2, waiting for transfers between devices, reduce_gradient(): return lax.psum_scatter(term_part, 'cuts', scatter_dimension=0, tiled=True)  69.8 us
    another operation x18, other arithmetic  50.1 us
    dot_general x6, matrix products, place_patches(): jnp.einsum('hfi,fscik->schk', row_onehot, placed_cols, preferred_element_...  49.4 us
    dot_general x16, matrix products, right_product(): jnp.einsum('fcij,cjdk->fdik', field.astype(jnp.bfloat16), table, preferre...  45.2 us
    all_gather x2, blocking collectives, body(): lax.all_gather(current.astype(jnp.bfloat16), 'cuts', axis=0, tiled=True)  26.2 us
    unnamed x49, local copies, waits for them, and re-layouts  15.1 us
    ppermute x4, starting transfers between devices, passed_along(): return lax.ppermute(x, axis, pairs)  13.5 us
  transfers between devices with their start and end apart: 7, of which 5 were waited for; matrix products, arithmetic and copies ran while one was open for 21% of the time, Pallas kernels for 0%

commit v1 on v0

v1 whole, which is shorter than its diff:
```python
import functools
import math

import jax
import jax.numpy as jnp
import ml_dtypes
import numpy as np
from jax import lax
from jax.experimental import pallas as pl
from jax.experimental.pallas import tpu as pltpu
from jax.sharding import PartitionSpec as P

ITERS = 2
STEP_SIZE = 0.05
AMPLITUDE_FLOOR = 0.25
GROUP = 4


def base_tables(side):
    index = np.arange(side)
    angle = (index[:, None] * index[None, :] % side) * (2.0 * math.pi / side)
    four = np.exp(-1j * angle) / math.sqrt(side)
    centred = (index + side // 2) % side - side // 2
    chirp = np.exp(-1j * math.pi * centred * centred / (4.0 * side))
    first_row = np.array(
        [np.sum(chirp * np.exp(2j * math.pi * index * shift / side)) for shift in range(side)]
    ) / side
    first_row = 0.5 * (first_row + first_row[(-index) % side])
    prop = first_row[(index[:, None] - index[None, :]) % side]
    planes = np.stack([prop.real, prop.imag, four.real, four.imag])
    return planes.astype(ml_dtypes.bfloat16)


def prep_kernel(pos_ref, amp_ref, out_ref, meta_ref, half_ref, src_ref):
    tile_count = lax.axis_size("tile")
    cut_count = lax.axis_size("cuts")
    tile = lax.axis_index("tile")
    cut = lax.axis_index("cuts")
    held = amp_ref.shape[0]
    capacity = out_ref.shape[0] // tile_count
    total = pos_ref.shape[0] // 2
    load = 2 * held
    width = amp_ref.shape[-1]
    for frame in range(held):
        half_ref[frame] = amp_ref[frame].astype(jnp.bfloat16)

    def clear(slot, carry):
        src_ref[slot] = 0
        return carry

    lax.fori_loop(0, out_ref.shape[0], clear, 0)
    start = (tile * cut_count + cut) * held
    owners = [pos_ref[total + start + frame] // width for frame in range(held)]
    for frame in range(held):
        slot = jnp.int32(0)
        for earlier in range(frame):
            slot = slot + (owners[earlier] == owners[frame]).astype(jnp.int32)
        src_ref[owners[frame] * capacity + slot] = frame

    def fill(slot, carry):
        out_ref[slot] = half_ref[src_ref[slot]]
        return carry

    lax.fori_loop(0, out_ref.shape[0], fill, 0)

    def scan(reader, count):
        first = count
        begin = (reader * cut_count + cut) * held
        for frame in range(held):
            col = pos_ref[total + begin + frame]
            meta_ref[count] = pos_ref[begin + frame]
            meta_ref[32 + count] = col - tile * width
            meta_ref[64 + count] = reader * capacity + count - first
            count = count + (col // width == tile).astype(jnp.int32)
        return count

    count = lax.fori_loop(0, tile_count, scan, jnp.int32(0))

    def tidy(slot, carry):
        live = slot < count
        for field in range(3):
            meta_ref[32 * field + slot] = jnp.where(live, meta_ref[32 * field + slot], 0)
        return carry

    lax.fori_loop(0, load, tidy, 0)
    meta_ref[96] = count


def prepare(positions, amplitudes, tile_count, capacity):
    side = amplitudes.shape[-1]
    return pl.pallas_call(
        prep_kernel,
        out_shape=(
            jax.ShapeDtypeStruct((tile_count * capacity, side, side), jnp.bfloat16),
            jax.ShapeDtypeStruct((128,), jnp.int32),
        ),
        in_specs=[
            pl.BlockSpec(memory_space=pltpu.SMEM),
            pl.BlockSpec(memory_space=pltpu.VMEM),
        ],
        out_specs=(
            pl.BlockSpec(memory_space=pltpu.VMEM),
            pl.BlockSpec(memory_space=pltpu.SMEM),
        ),
        scratch_shapes=[
            pltpu.VMEM(amplitudes.shape, jnp.bfloat16),
            pltpu.SMEM((tile_count * capacity,), jnp.int32),
        ],
        name="prep",
    )(positions.T.reshape(-1), amplitudes)


def times(left, right):
    return left[0] * right[0] - left[1] * right[1], left[0] * right[1] + left[1] * right[0]


def conj_times(left, right):
    return left[0] * right[0] + left[1] * right[1], left[0] * right[1] - left[1] * right[0]


def two_sided(fields, right_table, left_table):
    side = fields[0][0].shape[-1]
    results = []
    for pair in range(0, len(fields), 2):
        rows = [
            jnp.concatenate([part.astype(jnp.bfloat16) for part in field], axis=1)
            for field in fields[pair : pair + 2]
        ]
        first = jnp.dot(
            jnp.concatenate(rows, axis=0), right_table, preferred_element_type=jnp.float32
        ).astype(jnp.bfloat16)
        turned = jnp.concatenate(
            [
                jnp.concatenate([first[:side, :side], first[side:, :side]], axis=1),
                jnp.concatenate([first[:side, side:], first[side:, side:]], axis=1),
            ],
            axis=0,
        )
        second = jnp.dot(left_table, turned, preferred_element_type=jnp.float32)
        results.append((second[:side, :side], second[side:, :side]))
        results.append((second[:side, side:], second[side:, side:]))
    return results


def frames_kernel(
    meta_ref, own_ref, next_ref, amp_ref, probe_ref, planes_ref, grad_ref, panel, tables, views, kept
):
    slices = own_ref.shape[0]
    side = own_ref.shape[-1]
    for level in range(slices):
        for part in range(2):
            plane = 2 * level + part
            panel[plane, 0] = own_ref[level, part].astype(jnp.float32)
            panel[plane, 1] = next_ref[level, part].astype(jnp.float32)
    grad_ref[...] = jnp.zeros_like(grad_ref)
    for kind in range(2):
        real, imag = planes_ref[2 * kind], planes_ref[2 * kind + 1]
        tables[2 * kind, :side, :side] = real
        tables[2 * kind, side:, side:] = real
        tables[2 * kind, :side, side:] = imag
        tables[2 * kind, side:, :side] = -imag
        tables[2 * kind + 1, :side, :side] = real
        tables[2 * kind + 1, side:, side:] = real
        tables[2 * kind + 1, :side, side:] = -imag
        tables[2 * kind + 1, side:, :side] = imag
    lane = lax.broadcasted_iota(jnp.int32, (side, side), 1)
    count = meta_ref[96]

    def group_step(group, carry):
        first = group * GROUP
        rows = [meta_ref[first + k] for k in range(GROUP)]
        cols = [meta_ref[32 + first + k] for k in range(GROUP)]
        for k in range(GROUP):
            from_own = lane >= cols[k]
            back_by = (side - cols[k]) % side
            for plane in range(2 * slices):
                joined = jnp.where(
                    from_own,
                    panel[plane, 0, pl.ds(rows[k], side), :],
                    panel[plane, 1, pl.ds(rows[k], side), :],
                )
                views[k, plane] = pltpu.roll(joined, back_by, 1)

        def view(k, level):
            return views[k, 2 * level], views[k, 2 * level + 1]

        def probe():
            return probe_ref[0], probe_ref[1]

        def add(k, level, patch):
            in_own = lane >= cols[k]
            for part in range(2):
                plane = 2 * level + part
                moved = pltpu.roll(patch[part], cols[k], 1)
                where_now = pl.ds(rows[k], side)
                grad_ref[0, plane, where_now, :] += jnp.where(in_own, moved, 0.0)
                grad_ref[1, plane, where_now, :] += jnp.where(in_own, 0.0, moved)

        members = range(GROUP)
        wave = [times(probe(), view(k, 0)) for k in members]
        for level in range(1, slices):
            moved = two_sided(wave, tables[0], tables[1])
            for k in members:
                kept[k, 2 * level - 2] = moved[k][0]
                kept[k, 2 * level - 1] = moved[k][1]
            wave = [times(view(k, level), moved[k]) for k in members]
        far = two_sided(wave, tables[2], tables[3])
        resid = []
        for k in members:
            real, imag = far[k]
            power = jnp.maximum(real * real + imag * imag, AMPLITUDE_FLOOR * AMPLITUDE_FLOOR)
            measured = amp_ref[meta_ref[64 + first + k]].astype(jnp.float32)
            live = jnp.where(first + k < count, 1.0, 0.0)
            factor = live - (live * measured) * lax.rsqrt(power)
            resid.append((real * factor, imag * factor))
        back = two_sided(resid, tables[3], tables[2])
        for level in range(slices - 1, 0, -1):
            for k in members:
                add(k, level, conj_times((kept[k, 2 * level - 2], kept[k, 2 * level - 1]), back[k]))
            back = two_sided(
                [conj_times(view(k, level), back[k]) for k in members], tables[1], tables[0]
            )
        for k in members:
            add(k, 0, conj_times(probe(), back[k]))
        return carry

    lax.fori_loop(0, (count + GROUP - 1) // GROUP, group_step, 0)


def frame_gradient(meta, own, following, measured, probe_field, planes):
    slices, _, height, side = own.shape
    vmem = pl.BlockSpec(memory_space=pltpu.VMEM)
    return pl.pallas_call(
        frames_kernel,
        out_shape=jax.ShapeDtypeStruct((2, 2 * slices, height, side), jnp.float32),
        in_specs=[pl.BlockSpec(memory_space=pltpu.SMEM)] + [vmem] * 5,
        out_specs=vmem,
        scratch_shapes=[
            pltpu.VMEM((2 * slices, 2, height, side), jnp.float32),
            pltpu.VMEM((4, 2 * side, 2 * side), jnp.bfloat16),
            pltpu.VMEM((GROUP, 2 * slices, side, side), jnp.float32),
            pltpu.VMEM((GROUP, 2 * slices - 2, side, side), jnp.float32),
        ],
        compiler_params=pltpu.CompilerParams(vmem_limit_bytes=48 << 20),
        cost_estimate=pl.CostEstimate(
            flops=16 * 16 * 2**24, bytes_accessed=6 << 20, transcendentals=16 * side * side
        ),
        name="frames",
    )(meta, own, following, measured, probe_field, planes)


def passed_along(x, axis, by):
    peers = lax.axis_size(axis)
    pairs = [(i, i + by) for i in range(peers) if 0 <= i + by < peers]
    return lax.ppermute(x, axis, pairs)


def body(amplitudes, positions, probe_field, object_slices):
    tile_count = lax.axis_size("tile")
    frames_held, side, _ = amplitudes.shape
    capacity = max(2, 2 * frames_held // tile_count)
    outgoing, meta = prepare(positions, amplitudes, tile_count, capacity)
    incoming = lax.all_to_all(
        outgoing.reshape(tile_count, capacity, side, side), "tile", split_axis=0, concat_axis=0, tiled=True
    ).reshape(tile_count * capacity, side, side)
    planes = jnp.asarray(base_tables(side))
    current = object_slices
    for turn in range(ITERS):
        stacked = lax.all_gather(current.astype(jnp.bfloat16), "cuts", axis=0, tiled=True)
        following = passed_along(stacked, "tile", -1)
        term = frame_gradient(meta, stacked, following, incoming, probe_field, planes)
        term = term.reshape((2,) + stacked.shape)
        moved = passed_along(term[1], "tile", 1)
        share = lax.psum_scatter(term[0] + moved, "cuts", scatter_dimension=0, tiled=True)
        current = current - STEP_SIZE * share
    return current


def solution(mesh):
    in_specs = (P(("tile", "cuts"), None, None), P(), P(), P("cuts", None, None, "tile"))
    out_specs = P("cuts", None, None, "tile")
    return jax.shard_map(body, mesh=mesh, in_specs=in_specs, out_specs=out_specs, check_vma=False)
```

time: 466 us -> 195 us (0.42)
  the two profiles are of different devices: /device:TPU:0 before, /device:TPU:10 now
where the time goes in v1:
time: 195 us; the launch traced here: 192 us
  waiting for transfers between devices  105 us (54%)
  blocking collectives  26.5 us (14%)
  Pallas kernels  21.1 us (11%)
  starting transfers between devices  19.5 us (10%)
  between operations  13.5 us (7%)
  other arithmetic  4.99 us (3%)
    reduce_scatter x2, waiting for transfers between devices, body(): lax.psum_scatter(term[0] + moved, 'cuts', scatter_dimension=0, tiled=True)  54.2 us
    ppermute x4, waiting for transfers between devices, passed_along(): return lax.ppermute(x, axis, pairs)  50.6 us
    all_gather x2, blocking collectives, body(): lax.all_gather(current.astype(jnp.bfloat16), 'cuts', axis=0, tiled=True)  26.5 us
    pallas_call x2, Pallas kernels, frame_gradient(): pl.pallas_call(frames_kernel, out_shape=jax.ShapeDtypeStruct((2, 2 * slic...  15.2 us
    ppermute x4, starting transfers between devices, passed_along(): return lax.ppermute(x, axis, pairs)  10.8 us
    all_to_all x1, starting transfers between devices, body(): lax.all_to_all(outgoing.reshape(tile_count, capacity, side, side), 'tile'...  8.61 us
    pallas_call x1, Pallas kernels, prepare(): pl.pallas_call(prep_kernel, out_shape=(jax.ShapeDtypeStruct((tile_count *...  5.92 us
  transfers between devices with their start and end apart: 7, of which 6 were waited for; matrix products, arithmetic and copies ran while one was open for 0% of the time, Pallas kernels for 0%

profile of v1, /device:TPU:10, one launch (start us, length us, event | category | flops | bytes accessed | tf_op | source)
XLA Modules:
  0.0 192.2 jit_solution(7276958385268169812)
XLA Ops:
  6.5 1.3 copy.8
  7.8 5.9 %prep.1 = (bf16[64,128,128]{2,1,0:T(8,128)(2,1)}, s32[128]{0:T(128)}) custom-call(s32[2048]{0:T(1024)} %bitcast.18, f32[8,128,128]{2,1,0:T(8,128)} %amp_ref.1), custom_call_target="tpu_custom_call" | custom-call | tf_op jit(solution)/shard_map/prep/pallas_call | solution.py:91
  13.8 0.0 copy-start.3
  13.8 0.0 copy-start
  13.8 0.0 copy-start.2
  13.8 8.6 %all-to-all-start = ((bf16[32,2,128,128]{3,2,1,0:T(8,128)(2,1)}), bf16[32,2,128,128]{3,2,1,0:T(8,128)(2,1)S(1)}, u32[]{:S(2)}, u32[]{:S(2)}) async-start(bf16[32,2,128,128]{3,2,1,0:T(8,128)(2,1)} %bitcast.15), calls=%async_computation | async-start | bytes 4194304 | tf_op jit(solution)/shard_map/all_to_all | solution.py:263
  22.4 0.0 reduce-scatter.3.cloned.1.call-start
  22.5 13.3 %all_gather.6.own_ref = bf16[4,2,256,128]{3,2,1,0:T(8,128)(2,1)S(1)} all-gather(bf16[1,2,256,128]{3,2,1,0:T(8,128)(2,1)S(1)} %convert_element_type.6), channel_id=1, replica_groups=mesh['tile'=32,'cuts'=4] {'cuts'}, dimensions={0}, use_global_device_ids=true | all-gather | bytes 655360 | tf_op jit(solution)/shard_map/all_gather | solution.py:269
  35.8 2.0 %collective-permute-start = (bf16[4,2,256,128]{3,2,1,0:T(8,128)(2,1)S(1)}, bf16[4,2,256,128]{3,2,1,0:T(8,128)(2,1)S(1)}, u32[]{:S(2)}, u32[]{:S(2)}) collective-permute-start(bf16[4,2,256,128]{3,2,1,0:T(8,128)(2,1)S(1)} %all_gather.6.own_ref), channel_id=1, source_target_pairs={{4,0},{8,4},{12,8},{16,12},{20,16},{24,20},{28,24},{32,28},{36,32}... | collective-permute-start | bytes 1572872 | tf_op jit(solution)/shard_map/ppermute | solution.py:255
  37.8 14.3 %collective-permute-done.next_ref = bf16[4,2,256,128]{3,2,1,0:T(8,128)(2,1)S(1)} collective-permute-done((bf16[4,2,256,128]{3,2,1,0:T(8,128)(2,1)S(1)}, bf16[4,2,256,128]{3,2,1,0:T(8,128)(2,1)S(1)}, u32[]{:S(2)}, u32[]{:S(2)}) %collective-permute-start) | collective-permute-done | bytes 524320 | tf_op jit(solution)/shard_map/ppermute | solution.py:255
  52.1 0.0 all-to-all-done
  52.1 0.0 copy-done.2
  52.1 7.6 %frames.2 = f32[2,8,256,128]{3,2,1,0:T(8,128)S(1)} custom-call(s32[128]{0:T(128)S(1)} %copy-done.1, bf16[4,2,256,128]{3,2,1,0:T(8,128)(2,1)S(1)} %all_gather.6.own_ref, bf16[4,2,256,128]{3,2,1,0:T(8,128)(2,1)S(1)} %collective-permute-done.next_ref, bf16[64,128,128]{2,1,0:T(8,128)(2,1)S(1)} %bitcast.11, f32[2,128,128]{2,1,0:T(8,128)S(1)} %copy-done, ...), custom_call_target="tpu_custom_call" | custom-call | flops 4294967296 | bytes 6291456 | tf_op jit(solution)/shard_map/frames/pallas_call | solution.py:233
  59.7 0.1 fusion.2
  59.9 2.9 %collective-permute-start.1 = (f32[4,2,256,128]{3,2,1,0:T(8,128)S(1)}, f32[4,2,256,128]{3,2,1,0:T(8,128)S(1)}, u32[]{:S(2)}, u32[]{:S(2)}) collective-permute-start(f32[4,2,256,128]{3,2,1,0:T(8,128)S(1)} %bitcast.16), channel_id=1, source_target_pairs={{0,4},{4,8},{8,12},{12,16},{16,20},{20,24},{24,28},{28,32},{32,36}... | collective-permute-start | bytes 3145736 | tf_op jit(solution)/shard_map/ppermute | solution.py:255
  62.8 15.3 %collective-permute-done.1 = f32[4,2,256,128]{3,2,1,0:T(8,128)S(1)} collective-permute-done((f32[4,2,256,128]{3,2,1,0:T(8,128)S(1)}, f32[4,2,256,128]{3,2,1,0:T(8,128)S(1)}, u32[]{:S(2)}, u32[]{:S(2)}) %collective-permute-start.1) | collective-permute-done | bytes 1048608 | tf_op jit(solution)/shard_map/ppermute | solution.py:255
  78.1 1.1 add.10
  79.3 0.0 reduce-scatter.3.cloned.1.call-update
  79.3 0.0 reduce-scatter.5.cloned.1.call-start
  79.3 26.4 %reduce-scatter.3.cloned.1.call-done = f32[1,2,256,128]{3,2,1,0:T(8,128)} async-done(((f32[4,2,256,128]{3,2,1,0:T(8,128)}), f32[1,2,256,128]{3,2,1,0:T(8,128)}) %reduce-scatter.3.cloned.1.call-update) | async-done | bytes 262160 | tf_op jit(solution)/shard_map/reduce_scatter | solution.py:274
  105.7 1.0 fusion
  106.7 13.3 %all_gather.7.own_ref = bf16[4,2,256,128]{3,2,1,0:T(8,128)(2,1)S(1)} all-gather(bf16[1,2,256,128]{3,2,1,0:T(8,128)(2,1)S(1)} %fusion), channel_id=1, replica_groups=mesh['tile'=32,'cuts'=4] {'cuts'}, dimensions={0}, use_global_device_ids=true | all-gather | bytes 655360 | tf_op jit(solution)/shard_map/all_gather | solution.py:269
  120.0 1.9 collective-permute-start.2
  121.9 6.7 %collective-permute-done.2.next_ref = bf16[4,2,256,128]{3,2,1,0:T(8,128)(2,1)S(1)} collective-permute-done((bf16[4,2,256,128]{3,2,1,0:T(8,128)(2,1)S(1)}, bf16[4,2,256,128]{3,2,1,0:T(8,128)(2,1)S(1)}, u32[]{:S(2)}, u32[]{:S(2)}) %collective-permute-start.2) | collective-permute-done | bytes 524320 | tf_op jit(solution)/shard_map/ppermute | solution.py:255
  128.6 7.6 %frames.3 = f32[2,8,256,128]{3,2,1,0:T(8,128)S(1)} custom-call(s32[128]{0:T(128)S(1)} %copy-done.1, bf16[4,2,256,128]{3,2,1,0:T(8,128)(2,1)S(1)} %all_gather.7.own_ref, bf16[4,2,256,128]{3,2,1,0:T(8,128)(2,1)S(1)} %collective-permute-done.2.next_ref, bf16[64,128,128]{2,1,0:T(8,128)(2,1)S(1)} %bitcast.12, f32[2,128,128]{2,1,0:T(8,128)S(1)} %copy-done, ...), custom_call_target="tpu_custom_call" | custom-call | flops 4294967296 | bytes 6291456 | tf_op jit(solution)/shard_map/frames/pallas_call | solution.py:233
  136.2 0.2 fusion.1
  136.4 3.9 %collective-permute-start.3 = (f32[4,2,256,128]{3,2,1,0:T(8,128)S(1)}, f32[4,2,256,128]{3,2,1,0:T(8,128)S(1)}, u32[]{:S(2)}, u32[]{:S(2)}) collective-permute-start(f32[4,2,256,128]{3,2,1,0:T(8,128)S(1)} %bitcast.17), channel_id=1, source_target_pairs={{0,4},{4,8},{8,12},{12,16},{16,20},{20,24},{24,28},{28,32},{32,36}... | collective-permute-start | bytes 3145736 | tf_op jit(solution)/shard_map/ppermute | solution.py:255
  140.3 14.3 %collective-permute-done.3 = f32[4,2,256,128]{3,2,1,0:T(8,128)S(1)} collective-permute-done((f32[4,2,256,128]{3,2,1,0:T(8,128)S(1)}, f32[4,2,256,128]{3,2,1,0:T(8,128)S(1)}, u32[]{:S(2)}, u32[]{:S(2)}) %collective-permute-start.3) | collective-permute-done | bytes 1048608 | tf_op jit(solution)/shard_map/ppermute | solution.py:255
  154.6 1.1 add.11
  155.7 0.0 reduce-scatter.5.cloned.1.call-update
  155.7 27.9 %reduce-scatter.5.cloned.1.call-done = f32[1,2,256,128]{3,2,1,0:T(8,128)} async-done(((f32[4,2,256,128]{3,2,1,0:T(8,128)}), f32[1,2,256,128]{3,2,1,0:T(8,128)}) %reduce-scatter.5.cloned.1.call-update) | async-done | bytes 262160 | tf_op jit(solution)/shard_map/reduce_scatter | solution.py:274
  183.6 1.7 multiply_subtract_fusion
  (9 shorter events, 0.0 us)
Async XLA Ops:
  13.8 8.7 %copy-start.3 = (f32[1,2,256,128]{3,2,1,0:T(8,128)S(1)}, f32[1,2,256,128]{3,2,1,0:T(8,128)}, u32[]{:S(2)}) copy-start(f32[1,2,256,128]{3,2,1,0:T(8,128)} %param.8) | copy-start | bytes 786436
  13.8 38.3 %copy-start = (f32[2,128,128]{2,1,0:T(8,128)S(1)}, f32[2,128,128]{2,1,0:T(8,128)}, u32[]{:S(2)}) copy-start(f32[2,128,128]{2,1,0:T(8,128)} %probe_ref.3) | copy-start | bytes 393220
  13.8 38.3 %copy-start.1 = (s32[128]{0:T(128)S(1)}, s32[128]{0:T(128)}, u32[]{:S(2)}) copy-start(s32[128]{0:T(128)} %get-tuple-element.7.meta_ref) | copy-start | bytes 1540
  13.8 38.3 %copy-start.2 = (bf16[4,128,128]{2,1,0:T(8,128)(2,1)S(1)}, bf16[4,128,128]{2,1,0:T(8,128)(2,1)}, u32[]{:S(2)}) copy-start(bf16[4,128,128]{2,1,0:T(8,128)(2,1)} %constant.4.clone.planes_ref) | copy-start | bytes 393220
  13.8 38.3 %all-to-all-start = ((bf16[32,2,128,128]{3,2,1,0:T(8,128)(2,1)}), bf16[32,2,128,128]{3,2,1,0:T(8,128)(2,1)S(1)}, u32[]{:S(2)}, u32[]{:S(2)}) async-start(bf16[32,2,128,128]{3,2,1,0:T(8,128)(2,1)} %bitcast.15), calls=%async_computation | async-start | bytes 4194304 | tf_op jit(solution)/shard_map/all_to_all | solution.py:263
  22.4 83.3 %reduce-scatter.3.cloned.1.call-start = ((), (), s32[]{:S(2)}) async-start(), calls=%async_computation.3 | async-start | bytes 1310720 | tf_op jit(solution)/shard_map/reduce_scatter | solution.py:274
  35.8 16.3 %collective-permute-start = (bf16[4,2,256,128]{3,2,1,0:T(8,128)(2,1)S(1)}, bf16[4,2,256,128]{3,2,1,0:T(8,128)(2,1)S(1)}, u32[]{:S(2)}, u32[]{:S(2)}) collective-permute-start(bf16[4,2,256,128]{3,2,1,0:T(8,128)(2,1)S(1)} %all_gather.6.own_ref), channel_id=1, source_target_pairs={{4,0},{8,4},{12,8},{16,12},{20,16},{24,20},{28,24},{32,28},{36,32}... | collective-permute-start | bytes 1572872 | tf_op jit(solution)/shard_map/ppermute | solution.py:255
  59.9 18.2 %collective-permute-start.1 = (f32[4,2,256,128]{3,2,1,0:T(8,128)S(1)}, f32[4,2,256,128]{3,2,1,0:T(8,128)S(1)}, u32[]{:S(2)}, u32[]{:S(2)}) collective-permute-start(f32[4,2,256,128]{3,2,1,0:T(8,128)S(1)} %bitcast.16), channel_id=1, source_target_pairs={{0,4},{4,8},{8,12},{12,16},{16,20},{20,24},{24,28},{28,32},{32,36}... | collective-permute-start | bytes 3145736 | tf_op jit(solution)/shard_map/ppermute | solution.py:255
  78.1 27.6 %copy-start.4 = (f32[1,2,256,128]{3,2,1,0:T(8,128)S(1)}, f32[1,2,256,128]{3,2,1,0:T(8,128)}, u32[]{:S(2)}) copy-start(f32[1,2,256,128]{3,2,1,0:T(8,128)} %param.8) | copy-start | bytes 786436
  79.3 104.3 %reduce-scatter.5.cloned.1.call-start = ((), (), s32[]{:S(2)}) async-start(), calls=%async_computation.4 | async-start | bytes 1310720 | tf_op jit(solution)/shard_map/reduce_scatter | solution.py:274
  120.0 8.6 %collective-permute-start.2 = (bf16[4,2,256,128]{3,2,1,0:T(8,128)(2,1)S(1)}, bf16[4,2,256,128]{3,2,1,0:T(8,128)(2,1)S(1)}, u32[]{:S(2)}, u32[]{:S(2)}) collective-permute-start(bf16[4,2,256,128]{3,2,1,0:T(8,128)(2,1)S(1)} %all_gather.7.own_ref), channel_id=1, source_target_pairs={{4,0},{8,4},{12,8},{16,12},{20,16},{24,20},{28,24},{32,28},{36,32}... | collective-permute-start | bytes 1572872 | tf_op jit(solution)/shard_map/ppermute | solution.py:255
  136.4 18.2 %collective-permute-start.3 = (f32[4,2,256,128]{3,2,1,0:T(8,128)S(1)}, f32[4,2,256,128]{3,2,1,0:T(8,128)S(1)}, u32[]{:S(2)}, u32[]{:S(2)}) collective-permute-start(f32[4,2,256,128]{3,2,1,0:T(8,128)S(1)} %bitcast.17), channel_id=1, source_target_pairs={{0,4},{4,8},{8,12},{12,16},{16,20},{20,24},{24,28},{28,32},{32,36}... | collective-permute-start | bytes 3145736 | tf_op jit(solution)/shard_map/ppermute | solution.py:255
  154.6 29.0 %copy-start.5 = (f32[1,2,256,128]{3,2,1,0:T(8,128)S(1)}, f32[1,2,256,128]{3,2,1,0:T(8,128)}, u32[]{:S(2)}) copy-start(f32[1,2,256,128]{3,2,1,0:T(8,128)} %reduce-scatter.3.cloned.1.call-done) | copy-start | bytes 786436
Sparse Core Ops, SparseCore 0:
  79.4 26.2 reduce-scatter.2
  155.8 27.6 reduce-scatter.4

commit v2 on v1

--- a/solution.py
+++ b/solution.py
@@ -31,83 +31,314 @@
     return planes.astype(ml_dtypes.bfloat16)
 
 
-def prep_kernel(pos_ref, amp_ref, out_ref, meta_ref, half_ref, src_ref):
+def slots_kernel(pos_ref, amp_ref, out_ref, half_ref, src_ref):
     tile_count = lax.axis_size("tile")
     cut_count = lax.axis_size("cuts")
-    tile = lax.axis_index("tile")
-    cut = lax.axis_index("cuts")
     held = amp_ref.shape[0]
     capacity = out_ref.shape[0] // tile_count
     total = pos_ref.shape[0] // 2
-    load = 2 * held
-    width = amp_ref.shape[-1]
+    shift = amp_ref.shape[-1].bit_length() - 1
     for frame in range(held):
         half_ref[frame] = amp_ref[frame].astype(jnp.bfloat16)
-
-    def clear(slot, carry):
+    for slot in range(out_ref.shape[0]):
         src_ref[slot] = 0
-        return carry
-
-    lax.fori_loop(0, out_ref.shape[0], clear, 0)
-    start = (tile * cut_count + cut) * held
-    owners = [pos_ref[total + start + frame] // width for frame in range(held)]
+    start = (lax.axis_index("tile") * cut_count + lax.axis_index("cuts")) * held
+    owners = [pos_ref[total + start + frame] >> shift for frame in range(held)]
     for frame in range(held):
         slot = jnp.int32(0)
         for earlier in range(frame):
             slot = slot + (owners[earlier] == owners[frame]).astype(jnp.int32)
         src_ref[owners[frame] * capacity + slot] = frame
-
-    def fill(slot, carry):
+    for slot in range(out_ref.shape[0]):
         out_ref[slot] = half_ref[src_ref[slot]]
-        return carry
-
-    lax.fori_loop(0, out_ref.shape[0], fill, 0)
-
-    def scan(reader, count):
-        first = count
-        begin = (reader * cut_count + cut) * held
-        for frame in range(held):
-            col = pos_ref[total + begin + frame]
-            meta_ref[count] = pos_ref[begin + frame]
-            meta_ref[32 + count] = col - tile * width
-            meta_ref[64 + count] = reader * capacity + count - first
-            count = count + (col // width == tile).astype(jnp.int32)
-        return count
-
-    count = lax.fori_loop(0, tile_count, scan, jnp.int32(0))
-
-    def tidy(slot, carry):
-        live = slot < count
-        for field in range(3):
-            meta_ref[32 * field + slot] = jnp.where(live, meta_ref[32 * field + slot], 0)
-        return carry
-
-    lax.fori_loop(0, load, tidy, 0)
-    meta_ref[96] = count
-
-
-def prepare(positions, amplitudes, tile_count, capacity):
+
+
+def fill_slots(flat_positions, amplitudes, tile_count, capacity):
     side = amplitudes.shape[-1]
     return pl.pallas_call(
-        prep_kernel,
-        out_shape=(
-            jax.ShapeDtypeStruct((tile_count * capacity, side, side), jnp.bfloat16),
-            jax.ShapeDtypeStruct((128,), jnp.int32),
-        ),
+        slots_kernel,
+        out_shape=jax.ShapeDtypeStruct((tile_count * capacity, side, side), jnp.bfloat16),
         in_specs=[
             pl.BlockSpec(memory_space=pltpu.SMEM),
             pl.BlockSpec(memory_space=pltpu.VMEM),
         ],
-        out_specs=(
-            pl.BlockSpec(memory_space=pltpu.VMEM),
-            pl.BlockSpec(memory_space=pltpu.SMEM),
-        ),
+        out_specs=pl.BlockSpec(memory_space=pltpu.VMEM),
         scratch_shapes=[
             pltpu.VMEM(amplitudes.shape, jnp.bfloat16),
             pltpu.SMEM((tile_count * capacity,), jnp.int32),
         ],
-        name="prep",
-    )(positions.T.reshape(-1), amplitudes)
+        name="slots",
+    )(flat_positions, amplitudes)
+
+
+def list_kernel(held, shift, capacity, pos_ref, meta_ref):
+    tile_count = lax.axis_size("tile")
+    cut_count = lax.axis_size("cuts")
+    tile = lax.axis_index("tile")
+    cut = lax.axis_index("cuts")
+    total = pos_ref.shape[0] // 2
+    load = 2 * held
+
+    def scan(reader, count):
+        begin = (reader * cut_count + cut) * held
+        for frame in range(held):
+            meta_ref[64 + count] = reader * held + frame
+            count = count + ((pos_ref[total + begin + frame] >> shift) == tile).astype(jnp.int32)
+        return count
+
+    count = lax.fori_loop(0, tile_count, scan, jnp.int32(0))
+    before, slot = jnp.int32(-1), jnp.int32(0)
+    for rank in range(load):
+        live = rank < count
+        packed = jnp.where(live, meta_ref[64 + rank], 0)
+        reader = packed // held
+        frame = reader * cut_count * held + cut * held + packed % held
+        slot = jnp.where(reader == before, slot + 1, 0)
+        before = reader
+        meta_ref[rank] = jnp.where(live, pos_ref[frame], 0)
+        meta_ref[32 + rank] = jnp.where(live, pos_ref[total + frame] - (tile << shift), 0)
+        meta_ref[64 + rank] = jnp.where(live, reader * capacity + slot, 0)
+    meta_ref[96] = count
+
+
+def list_frames(flat_positions, held, side, capacity):
+    return pl.pallas_call(
+        functools.partial(list_kernel, held, side.bit_length() - 1, capacity),
+        out_shape=jax.ShapeDtypeStruct((128,), jnp.int32),
+        in_specs=[pl.BlockSpec(memory_space=pltpu.SMEM)],
+        out_specs=pl.BlockSpec(memory_space=pltpu.SMEM),
+        name="listing",
+    )(flat_positions)
+
+
+def exchange_kernel(reduces, gathers, *refs):
+    refs = list(refs)
+    term_ref = refs.pop(0) if reduces else None
+    held_ref = refs.pop(0)
+    new_ref = refs.pop(0) if reduces else None
+    own_ref, next_ref = (refs.pop(0), refs.pop(0)) if gathers else (None, None)
+    if reduces:
+        out_box, in_box, far_out, far_in, near_out, near_in = refs[:6]
+        tile_send, tile_recv, cut_send, cut_recv = refs[6:10]
+        refs = refs[10:]
+    if gathers:
+        rim_send, rim_recv, ring_send, ring_recv = refs
+    tile_count = lax.axis_size("tile")
+    tile = lax.axis_index("tile")
+    me = lax.axis_index("cuts")
+    peers = 4
+    right, left, across = (me + 1) % peers, (me + 3) % peers, (me + 2) % peers
+    has_next = tile < tile_count - 1
+    has_prev = tile > 0
+    barrier = pltpu.get_barrier_semaphore()
+
+    def greet(to_tile, to_cut):
+        pl.semaphore_signal(
+            barrier,
+            inc=1,
+            device_id={"tile": to_tile, "cuts": to_cut},
+            device_id_type=pl.DeviceIdType.MESH,
+        )
+
+    greet(tile, right)
+    greet(tile, left)
+
+    @pl.when(has_next)
+    def _():
+        greet(tile + 1, me)
+
+    @pl.when(has_prev)
+    def _():
+        greet(tile - 1, me)
+
+    def to_cut(source, target, sends, recvs, index, cut):
+        return pltpu.make_async_remote_copy(
+            src_ref=source,
+            dst_ref=target,
+            send_sem=sends.at[index],
+            recv_sem=recvs.at[index],
+            device_id={"tile": tile, "cuts": cut},
+            device_id_type=pl.DeviceIdType.MESH,
+        )
+
+    def to_tile(source, target, sends, recvs, index, by):
+        return pltpu.make_async_remote_copy(
+            src_ref=source,
+            dst_ref=target,
+            send_sem=sends.at[index],
+            recv_sem=recvs.at[index],
+            device_id={"tile": tile + by, "cuts": me},
+            device_id_type=pl.DeviceIdType.MESH,
+        )
+
+    def all_arrived():
+        pl.semaphore_wait(barrier, 2 + has_next.astype(jnp.int32) + has_prev.astype(jnp.int32))
+
+    def plane(half, level, part):
+        return term_ref[half, 2 * level + part]
+
+    if reduces:
+        order = [across, right, left, me]
+        forward = [
+            to_tile(out_box.at[k], in_box.at[k], tile_send, tile_recv, k, 1) for k in range(peers)
+        ]
+
+        @pl.when(has_next)
+        def _():
+            for k in range(peers):
+                for part in range(2):
+                    out_box[k, part] = plane(1, order[k], part).astype(jnp.bfloat16)
+
+        @pl.when(jnp.logical_not(has_prev))
+        def _():
+            in_box[...] = jnp.zeros_like(in_box)
+
+        all_arrived()
+
+        @pl.when(has_next)
+        def _():
+            for copy in forward:
+                copy.start()
+
+        def arrived(k):
+            @pl.when(has_prev)
+            def _():
+                forward[k].wait_recv()
+
+        def joined(k, part):
+            return plane(0, order[k], part) + in_box[k, part].astype(jnp.float32)
+
+        arrived(0)
+        far_out[0] = joined(0, 0).astype(jnp.bfloat16)
+        far_out[1] = joined(0, 1).astype(jnp.bfloat16)
+        far_right = to_cut(far_out.at[0], far_in.at[0], cut_send, cut_recv, 0, right)
+        far_left = to_cut(far_out.at[1], far_in.at[1], cut_send, cut_recv, 1, left)
+        far_right.start()
+        far_left.start()
+        near_right = to_cut(near_out.at[0], near_in.at[0], cut_send, cut_recv, 2, right)
+        near_left = to_cut(near_out.at[1], near_in.at[1], cut_send, cut_recv, 3, left)
+        arrived(1)
+        near_out[0, 1] = joined(1, 1).astype(jnp.bfloat16)
+        far_right.wait_recv()
+        near_out[0, 0] = (joined(1, 0) + far_in[0].astype(jnp.float32)).astype(jnp.bfloat16)
+        near_right.start()
+        arrived(2)
+        near_out[1, 0] = joined(2, 0).astype(jnp.bfloat16)
+        far_left.wait_recv()
+        near_out[1, 1] = (joined(2, 1) + far_in[1].astype(jnp.float32)).astype(jnp.bfloat16)
+        near_left.start()
+        arrived(3)
+        for part in range(2):
+            new_ref[0, part] = joined(3, part)
+        near_right.wait_recv()
+        near_left.wait_recv()
+        for part in range(2):
+            share = (
+                new_ref[0, part]
+                + near_in[0, part].astype(jnp.float32)
+                + near_in[1, part].astype(jnp.float32)
+            )
+            fresh = held_ref[0, part] - STEP_SIZE * share
+            new_ref[0, part] = fresh
+            if gathers:
+                own_ref[me, part] = fresh.astype(jnp.bfloat16)
+    else:
+        for part in range(2):
+            own_ref[me, part] = held_ref[0, part].astype(jnp.bfloat16)
+        all_arrived()
+
+    if gathers:
+
+        def ring(index, level, part, cut):
+            spot = own_ref.at[level] if part is None else own_ref.at[level, part]
+            return to_cut(spot, spot, ring_send, ring_recv, index, cut)
+
+        def rim(index, level):
+            return to_tile(own_ref.at[level], next_ref.at[level], rim_send, rim_recv, index, -1)
+
+        go_right, go_left = ring(0, me, None, right), ring(1, me, None, left)
+        from_left, from_right = ring(0, left, None, right), ring(1, right, None, left)
+        on_right, on_left = ring(2, left, 0, right), ring(3, right, 1, left)
+        far_first, far_second = ring(2, across, 0, right), ring(3, across, 1, left)
+        rims = [rim(0, me), rim(1, left), rim(2, right), rim(3, across)]
+
+        def pass_rim(k):
+            @pl.when(has_prev)
+            def _():
+                rims[k].start()
+
+        go_right.start()
+        go_left.start()
+        pass_rim(0)
+        from_left.wait_recv()
+        on_right.start()
+        pass_rim(1)
+        from_right.wait_recv()
+        on_left.start()
+        pass_rim(2)
+        far_first.wait_recv()
+        far_second.wait_recv()
+        pass_rim(3)
+
+        @pl.when(has_next)
+        def _():
+            for copy in rims:
+                copy.wait_recv()
+
+        @pl.when(jnp.logical_not(has_next))
+        def _():
+            next_ref[...] = jnp.zeros_like(next_ref)
+
+        for copy in (go_right, go_left, on_right, on_left):
+            copy.wait_send()
+
+        @pl.when(has_prev)
+        def _():
+            for copy in rims:
+                copy.wait_send()
+
+    if reduces:
+        for copy in (far_right, far_left, near_right, near_left):
+            copy.wait_send()
+
+        @pl.when(has_next)
+        def _():
+            for copy in forward:
+                copy.wait_send()
+
+
+def exchange(term, held, gathers, number):
+    reduces = term is not None
+    _, parts, height, width = held.shape
+    peers = lax.axis_size("cuts")
+    slices = peers
+    vmem = pl.BlockSpec(memory_space=pltpu.VMEM)
+    outs, scratch = [], []
+    if reduces:
+        outs.append(jax.ShapeDtypeStruct(held.shape, jnp.float32))
+        scratch += [
+            pltpu.VMEM((peers, parts, height, width), jnp.bfloat16),
+            pltpu.VMEM((peers, parts, height, width), jnp.bfloat16),
+            pltpu.VMEM((2, height, width), jnp.bfloat16),
+            pltpu.VMEM((2, height, width), jnp.bfloat16),
+            pltpu.VMEM((2, parts, height, width), jnp.bfloat16),
+            pltpu.VMEM((2, parts, height, width), jnp.bfloat16),
+        ] + [pltpu.SemaphoreType.DMA((4,))] * 4
+    if gathers:
+        outs += [jax.ShapeDtypeStruct((slices, parts, height, width), jnp.bfloat16)] * 2
+        scratch += [pltpu.SemaphoreType.DMA((4,))] * 4
+    operands = ([term] if reduces else []) + [held]
+    return pl.pallas_call(
+        functools.partial(exchange_kernel, reduces, gathers),
+        out_shape=tuple(outs),
+        in_specs=[vmem] * len(operands),
+        out_specs=tuple([vmem] * len(outs)),
+        scratch_shapes=scratch,
+        compiler_params=pltpu.CompilerParams(
+            collective_id=number, has_side_effects=True, vmem_limit_bytes=40 << 20
+        ),
+        name="exchange",
+    )(*operands)
 
 
 def times(left, right):
@@ -249,30 +480,25 @@
     )(meta, own, following, measured, probe_field, planes)
 
 
-def passed_along(x, axis, by):
-    peers = lax.axis_size(axis)
-    pairs = [(i, i + by) for i in range(peers) if 0 <= i + by < peers]
-    return lax.ppermute(x, axis, pairs)
-
-
 def body(amplitudes, positions, probe_field, object_slices):
     tile_count = lax.axis_size("tile")
     frames_held, side, _ = amplitudes.shape
     capacity = max(2, 2 * frames_held // tile_count)
-    outgoing, meta = prepare(positions, amplitudes, tile_count, capacity)
+    flat_positions = positions.T.reshape(-1)
+    outgoing = fill_slots(flat_positions, amplitudes, tile_count, capacity)
     incoming = lax.all_to_all(
         outgoing.reshape(tile_count, capacity, side, side), "tile", split_axis=0, concat_axis=0, tiled=True
     ).reshape(tile_count * capacity, side, side)
+    meta = list_frames(flat_positions, frames_held, side, capacity)
     planes = jnp.asarray(base_tables(side))
+    own, following = exchange(None, object_slices, True, 1)
     current = object_slices
     for turn in range(ITERS):
-        stacked = lax.all_gather(current.astype(jnp.bfloat16), "cuts", axis=0, tiled=True)
-        following = passed_along(stacked, "tile", -1)
-        term = frame_gradient(meta, stacked, following, incoming, probe_field, planes)
-        term = term.reshape((2,) + stacked.shape)
-        moved = passed_along(term[1], "tile", 1)
-        share = lax.psum_scatter(term[0] + moved, "cuts", scatter_dimension=0, tiled=True)
-        current = current - STEP_SIZE * share
+        term = frame_gradient(meta, own, following, incoming, probe_field, planes)
+        if turn < ITERS - 1:
+            current, own, following = exchange(term, current, True, 2 + turn)
+        else:
+            (current,) = exchange(term, current, False, 2 + turn)
     return current
 
 

time: 195 us -> 120 us (0.62); the launches traced: 192 us -> 119 us
  waiting for transfers between devices: 105 us -> 0.01 us
  Pallas kernels: 21.1 us -> 107 us
  blocking collectives: 26.5 us -> 0 us
  between operations: 13.5 us -> 0.11 us
  starting transfers between devices: 19.5 us -> 8.6 us
  other arithmetic: 4.99 us -> 0 us
    pallas_call x1 -> x5, Pallas kernels: 5.92 us -> 98.5 us  [the longest x3 93.5 us: exchange(): pl.pallas_call(functools.partial(exchange_kernel, reduces, gathers), out_...]
    reduce_scatter x2 -> x0, waiting for transfers between devices: 54.2 us -> none  [body(): lax.psum_scatter(term[0] + moved, 'cuts', scatter_dimension=0, tiled=True)]
    ppermute x4 -> x0, waiting for transfers between devices: 50.6 us -> none  [passed_along(): return lax.ppermute(x, axis, pairs)]
    all_gather x2 -> x0, blocking collectives: 26.5 us -> none  [body(): lax.all_gather(current.astype(jnp.bfloat16), 'cuts', axis=0, tiled=True)]
    ppermute x4 -> x0, starting transfers between devices: 10.8 us -> none  [passed_along(): return lax.ppermute(x, axis, pairs)]
    pallas_call x2, Pallas kernels: 15.2 us -> 8.56 us  [frame_gradient(): pl.pallas_call(frames_kernel, out_shape=jax.ShapeDtypeStruct((2, 2 * slic...]
    unnamed x13 -> x12, local copies, waits for them, and re-layouts: 1.33 us -> 3.58 us
    add x2 -> x0, other arithmetic: 2.23 us -> none  [body(): term[0] + moved]
  transfers between devices with their start and end apart: 7 -> 1, of which waited for: 6 -> 0; matrix products, arithmetic and copies ran while one was open for 0% -> 0% of each run, Pallas kernels for 0% -> 25%
where the time goes in v2:
time: 120 us; the launch traced here: 119 us
  Pallas kernels  107 us (89%)
  starting transfers between devices  8.6 us (7%)
  local copies, waits for them, and re-layouts  3.58 us (3%)
    pallas_call x3, Pallas kernels, exchange(): pl.pallas_call(functools.partial(exchange_kernel, reduces, gathers), out_...  93.5 us
    all_to_all x1, starting transfers between devices, body(): lax.all_to_all(outgoing.reshape(tile_count, capacity, side, side), 'tile'...  8.6 us
    pallas_call x2, Pallas kernels, frame_gradient(): pl.pallas_call(frames_kernel, out_shape=jax.ShapeDtypeStruct((2, 2 * slic...  8.56 us
    unnamed x12, local copies, waits for them, and re-layouts  3.58 us
    pallas_call x1, Pallas kernels, fill_slots(): pl.pallas_call(slots_kernel, out_shape=jax.ShapeDtypeStruct((tile_count *...  2.61 us
    pallas_call x1, Pallas kernels, list_frames(): pl.pallas_call(functools.partial(list_kernel, held, side.bit_length() - 1...  2.41 us
  transfers between devices with their start and end apart: 1, of which 0 were waited for; matrix products, arithmetic and copies ran while one was open for 0% of the time, Pallas kernels for 25%

profile of v2, /device:TPU:10, one launch (start us, length us, event | category | flops | bytes accessed | tf_op | source)
XLA Modules:
  0.0 119.4 jit_solution(11683694818623058312)
XLA Ops:
  0.0 1.3 %copy.8 = s32[1,8,2,128]{3,1,2,0:T(8,128)} copy(s32[1,8,2,128]{3,2,1,0:T(2,128)} %bitcast.12) | data formatting | bytes 16384
  1.3 2.6 %slots.1 = bf16[64,128,128]{2,1,0:T(8,128)(2,1)} custom-call(s32[2048]{0:T(1024)} %bitcast.10, f32[8,128,128]{2,1,0:T(8,128)} %amp_ref.1), custom_call_target="tpu_custom_call" | custom-call | tf_op jit(solution)/shard_map/slots/pallas_call | solution.py:58
  3.9 0.0 copy-start
  3.9 0.0 copy-start.2
  3.9 8.6 %all-to-all-start = ((bf16[32,2,128,128]{3,2,1,0:T(8,128)(2,1)}), bf16[32,2,128,128]{3,2,1,0:T(8,128)(2,1)S(1)}, u32[]{:S(2)}, u32[]{:S(2)}) async-start(bf16[32,2,128,128]{3,2,1,0:T(8,128)(2,1)} %bitcast.9), calls=%async_computation | async-start | bytes 4194304 | tf_op jit(solution)/shard_map/all_to_all | solution.py:489
  12.5 2.4 %listing.1.meta_ref = s32[128]{0:T(128)} custom-call(s32[2048]{0:T(1024)} %bitcast.11), custom_call_target="tpu_custom_call" | custom-call | tf_op jit(solution)/shard_map/listing/pallas_call | solution.py:105
  14.9 0.0 copy-done
  14.9 27.4 %exchange.3 = (bf16[4,2,256,128]{3,2,1,0:T(8,128)(2,1)S(1)}, bf16[4,2,256,128]{3,2,1,0:T(8,128)(2,1)S(1)}) custom-call(f32[1,2,256,128]{3,2,1,0:T(8,128)S(1)} %copy-done), custom_call_target="tpu_custom_call" | custom-call | tf_op jit(solution)/shard_map/exchange/pallas_call | solution.py:331
  42.4 0.0 all-to-all-done
  42.4 0.0 copy-done.2
  42.4 0.0 copy-start.1
  42.4 0.7 copy-done.1
  43.0 0.0 copy-start.3
  43.0 0.9 copy-done.3
  44.0 4.3 %frames.2.refs_0_ = f32[2,8,256,128]{3,2,1,0:T(8,128)S(1)} custom-call(s32[128]{0:T(128)S(1)} %copy-done.1, bf16[4,2,256,128]{3,2,1,0:T(8,128)(2,1)S(1)} %get-tuple-element.10.own_ref, bf16[4,2,256,128]{3,2,1,0:T(8,128)(2,1)S(1)} %get-tuple-element.11.next_ref, bf16[64,128,128]{2,1,0:T(8,128)(2,1)S(1)} %bitcast.7, f32[2,128,128]{2,1,0:T(8,128)S(1)} %copy-done.2, ...), custom_call_target="tpu_custom_call" | custom-call | flops 4294967296 | bytes 6291456 | tf_op jit(solution)/shard_map/frames/pallas_call | solution.py:464
  48.2 0.0 copy-start.4
  48.3 38.0 %exchange.4 = (f32[1,2,256,128]{3,2,1,0:T(8,128)S(1)}, bf16[4,2,256,128]{3,2,1,0:T(8,128)(2,1)S(1)}, bf16[4,2,256,128]{3,2,1,0:T(8,128)(2,1)S(1)}) custom-call(f32[2,8,256,128]{3,2,1,0:T(8,128)S(1)} %frames.2.refs_0_, f32[1,2,256,128]{3,2,1,0:T(8,128)S(1)} %copy-done), custom_call_target="tpu_custom_call" | custom-call | tf_op jit(solution)/shard_map/exchange/pallas_call | solution.py:331
  86.2 0.0 copy-done.4
  86.3 4.3 %frames.3.refs_0_ = f32[2,8,256,128]{3,2,1,0:T(8,128)S(1)} custom-call(s32[128]{0:T(128)S(1)} %copy-done.1, bf16[4,2,256,128]{3,2,1,0:T(8,128)(2,1)S(1)} %get-tuple-element.12.own_ref, bf16[4,2,256,128]{3,2,1,0:T(8,128)(2,1)S(1)} %get-tuple-element.13.next_ref, bf16[64,128,128]{2,1,0:T(8,128)(2,1)S(1)} %bitcast.8, f32[2,128,128]{2,1,0:T(8,128)S(1)} %copy-done.2, ...), custom_call_target="tpu_custom_call" | custom-call | flops 4294967296 | bytes 6291456 | tf_op jit(solution)/shard_map/frames/pallas_call | solution.py:464
  90.6 28.1 %exchange.5 = f32[1,2,256,128]{3,2,1,0:T(8,128)S(1)} custom-call(f32[2,8,256,128]{3,2,1,0:T(8,128)S(1)} %frames.3.refs_0_, f32[1,2,256,128]{3,2,1,0:T(8,128)S(1)} %get-tuple-element.14.refs_1_), custom_call_target="tpu_custom_call" | custom-call | tf_op jit(solution)/shard_map/exchange/pallas_call | solution.py:331
  118.7 0.7 copy.10
Async XLA Ops:
  3.9 11.0 %copy-start = (f32[1,2,256,128]{3,2,1,0:T(8,128)S(1)}, f32[1,2,256,128]{3,2,1,0:T(8,128)}, u32[]{:S(2)}) copy-start(f32[1,2,256,128]{3,2,1,0:T(8,128)} %refs_1_.1) | copy-start | bytes 786436
  3.9 38.5 %copy-start.2 = (f32[2,128,128]{2,1,0:T(8,128)S(1)}, f32[2,128,128]{2,1,0:T(8,128)}, u32[]{:S(2)}) copy-start(f32[2,128,128]{2,1,0:T(8,128)} %probe_ref.3) | copy-start | bytes 393220
  3.9 38.4 %all-to-all-start = ((bf16[32,2,128,128]{3,2,1,0:T(8,128)(2,1)}), bf16[32,2,128,128]{3,2,1,0:T(8,128)(2,1)S(1)}, u32[]{:S(2)}, u32[]{:S(2)}) async-start(bf16[32,2,128,128]{3,2,1,0:T(8,128)(2,1)} %bitcast.9), calls=%async_computation | async-start | bytes 4194304 | tf_op jit(solution)/shard_map/all_to_all | solution.py:489
  42.4 0.7 copy-start.1
  43.0 0.9 copy-start.3
  48.2 38.0 %copy-start.4 = (bf16[4,128,128]{2,1,0:T(8,128)(2,1)S(1)}, bf16[4,128,128]{2,1,0:T(8,128)(2,1)}, u32[]{:S(2)}) copy-start(bf16[4,128,128]{2,1,0:T(8,128)(2,1)} %constant.2.clone.planes_ref) | copy-start | bytes 393220

commit v3 on v1

--- a/solution.py
+++ b/solution.py
@@ -13,7 +13,8 @@
 ITERS = 2
 STEP_SIZE = 0.05
 AMPLITUDE_FLOOR = 0.25
-GROUP = 4
+GROUP = 8
+RING = 4
 
 
 def base_tables(side):
@@ -31,83 +32,436 @@
     return planes.astype(ml_dtypes.bfloat16)
 
 
-def prep_kernel(pos_ref, amp_ref, out_ref, meta_ref, half_ref, src_ref):
+def list_kernel(held, shift, capacity, pos_ref, meta_ref):
     tile_count = lax.axis_size("tile")
     cut_count = lax.axis_size("cuts")
     tile = lax.axis_index("tile")
     cut = lax.axis_index("cuts")
-    held = amp_ref.shape[0]
-    capacity = out_ref.shape[0] // tile_count
     total = pos_ref.shape[0] // 2
     load = 2 * held
-    width = amp_ref.shape[-1]
-    for frame in range(held):
-        half_ref[frame] = amp_ref[frame].astype(jnp.bfloat16)
-
-    def clear(slot, carry):
-        src_ref[slot] = 0
-        return carry
-
-    lax.fori_loop(0, out_ref.shape[0], clear, 0)
-    start = (tile * cut_count + cut) * held
-    owners = [pos_ref[total + start + frame] // width for frame in range(held)]
-    for frame in range(held):
-        slot = jnp.int32(0)
-        for earlier in range(frame):
-            slot = slot + (owners[earlier] == owners[frame]).astype(jnp.int32)
-        src_ref[owners[frame] * capacity + slot] = frame
-
-    def fill(slot, carry):
-        out_ref[slot] = half_ref[src_ref[slot]]
-        return carry
-
-    lax.fori_loop(0, out_ref.shape[0], fill, 0)
 
     def scan(reader, count):
-        first = count
         begin = (reader * cut_count + cut) * held
         for frame in range(held):
-            col = pos_ref[total + begin + frame]
-            meta_ref[count] = pos_ref[begin + frame]
-            meta_ref[32 + count] = col - tile * width
-            meta_ref[64 + count] = reader * capacity + count - first
-            count = count + (col // width == tile).astype(jnp.int32)
+            meta_ref[64 + count] = reader * held + frame
+            count = count + ((pos_ref[total + begin + frame] >> shift) == tile).astype(jnp.int32)
         return count
 
     count = lax.fori_loop(0, tile_count, scan, jnp.int32(0))
-
-    def tidy(slot, carry):
-        live = slot < count
-        for field in range(3):
-            meta_ref[32 * field + slot] = jnp.where(live, meta_ref[32 * field + slot], 0)
-        return carry
-
-    lax.fori_loop(0, load, tidy, 0)
+    before, slot = jnp.int32(-1), jnp.int32(0)
+    for rank in range(load):
+        live = rank < count
+        packed = jnp.where(live, meta_ref[64 + rank], 0)
+        reader = packed // held
+        frame = reader * cut_count * held + cut * held + packed % held
+        slot = jnp.where(reader == before, slot + 1, 0)
+        before = reader
+        meta_ref[rank] = jnp.where(live, pos_ref[frame], 0)
+        meta_ref[32 + rank] = jnp.where(live, pos_ref[total + frame] - (tile << shift), 0)
+        core, along_z, along_x = reader % 2, reader // 2 % RING, reader // (2 * RING)
+        line = jnp.where(core == 0, along_z * RING + along_x, (RING + along_x) * RING + along_z)
+        meta_ref[64 + rank] = jnp.where(live, line * capacity + slot, 0)
     meta_ref[96] = count
 
 
-def prepare(positions, amplitudes, tile_count, capacity):
-    side = amplitudes.shape[-1]
+def list_frames(flat_positions, held, side, capacity):
     return pl.pallas_call(
-        prep_kernel,
+        functools.partial(list_kernel, held, side.bit_length() - 1, capacity),
+        out_shape=jax.ShapeDtypeStruct((128,), jnp.int32),
+        in_specs=[pl.BlockSpec(memory_space=pltpu.SMEM)],
+        out_specs=pl.BlockSpec(memory_space=pltpu.SMEM),
+        name="listing",
+    )(flat_positions)
+
+
+def mesh_copy(source, target, send, recv, tile, cut):
+    return pltpu.make_async_remote_copy(
+        src_ref=source,
+        dst_ref=target,
+        send_sem=send,
+        recv_sem=recv,
+        device_id={"tile": tile, "cuts": cut},
+        device_id_type=pl.DeviceIdType.MESH,
+    )
+
+
+def greet(barrier, tile, cut):
+    pl.semaphore_signal(
+        barrier,
+        inc=1,
+        device_id={"tile": tile, "cuts": cut},
+        device_id_type=pl.DeviceIdType.MESH,
+    )
+
+
+def greet_near(barrier):
+    tile_count = lax.axis_size("tile")
+    tile = lax.axis_index("tile")
+    me = lax.axis_index("cuts")
+    has_next = tile < tile_count - 1
+    has_prev = tile > 0
+    greet(barrier, tile, (me + 1) % RING)
+    greet(barrier, tile, (me + 3) % RING)
+
+    @pl.when(has_next)
+    def _():
+        greet(barrier, tile + 1, me)
+
+    @pl.when(has_prev)
+    def _():
+        greet(barrier, tile - 1, me)
+
+    return 2 + has_next.astype(jnp.int32) + has_prev.astype(jnp.int32)
+
+
+def gather_steps(own_ref, next_ref, rim_send, rim_recv, ring_send, ring_recv):
+    tile_count = lax.axis_size("tile")
+    tile = lax.axis_index("tile")
+    me = lax.axis_index("cuts")
+    right, left, across = (me + 1) % RING, (me + 3) % RING, (me + 2) % RING
+    has_next = tile < tile_count - 1
+    has_prev = tile > 0
+
+    def ring(index, level, part, cut):
+        spot = own_ref.at[level] if part is None else own_ref.at[level, part]
+        return mesh_copy(spot, spot, ring_send.at[index], ring_recv.at[index], tile, cut)
+
+    def rim(index, level):
+        return mesh_copy(
+            own_ref.at[level], next_ref.at[level], rim_send.at[index], rim_recv.at[index], tile - 1, me
+        )
+
+    go_right, go_left = ring(0, me, None, right), ring(1, me, None, left)
+    from_left, from_right = ring(0, left, None, right), ring(1, right, None, left)
+    on_right, on_left = ring(2, left, 0, right), ring(3, right, 1, left)
+    far_first, far_second = ring(2, across, 0, right), ring(3, across, 1, left)
+    rims = [rim(0, me), rim(1, left), rim(2, right), rim(3, across)]
+
+    def pass_rim(k):
+        @pl.when(has_prev)
+        def _():
+            rims[k].start()
+
+    def begin():
+        go_right.start()
+        go_left.start()
+        pass_rim(0)
+
+    def take_left():
+        from_left.wait_recv()
+        on_right.start()
+        pass_rim(1)
+
+    def take_right():
+        from_right.wait_recv()
+        on_left.start()
+        pass_rim(2)
+
+    def take_across():
+        far_first.wait_recv()
+        far_second.wait_recv()
+        pass_rim(3)
+
+    def finish():
+        @pl.when(has_next)
+        def _():
+            for copy in rims:
+                copy.wait_recv()
+
+        @pl.when(jnp.logical_not(has_next))
+        def _():
+            next_ref[...] = jnp.zeros_like(next_ref)
+
+        for copy in (go_right, go_left, on_right, on_left):
+            copy.wait_send()
+
+        @pl.when(has_prev)
+        def _():
+            for copy in rims:
+                copy.wait_send()
+
+    return begin, take_left, take_right, take_across, finish
+
+
+def opening_kernel(
+    pos_ref, amp_ref, held_ref, own_ref, next_ref, inbox, mine, below, above, far, outbox,
+    line_send, line_recv, box_send, box_recv, rim_send, rim_recv, ring_send, ring_recv,
+):
+    cut_count = lax.axis_size("cuts")
+    tile = lax.axis_index("tile")
+    me = lax.axis_index("cuts")
+    held, side, _ = amp_ref.shape
+    shift = side.bit_length() - 1
+    total = pos_ref.shape[0] // 2
+    core = tile % 2
+    along_z = tile // 2 % RING
+    along_x = tile // (2 * RING)
+    first = (1 - core) * along_x + core * along_z
+    second = (1 - core) * along_z + core * along_x
+
+    def tile_at(first_at, second_at, target_core):
+        chip = (1 - core) * (first_at * RING + second_at) + core * (second_at * RING + first_at)
+        return chip * 2 + target_core
+
+    barrier = pltpu.get_barrier_semaphore()
+    expected = greet_near(barrier)
+    greet(barrier, tile_at(first, second, 1 - core), me)
+    for by in range(1, RING):
+        for target_core in range(2):
+            greet(barrier, tile_at((first + by) % RING, second, target_core), me)
+            greet(barrier, tile_at(first, (second + by) % RING, target_core), me)
+            expected = expected + 2
+    for part in range(2):
+        own_ref[me, part] = held_ref[0, part].astype(jnp.bfloat16)
+    for frame in range(held):
+        mine[frame] = amp_ref[frame].astype(jnp.bfloat16)
+    pl.semaphore_wait(barrier, expected + 1)
+
+    half = held // 2
+
+    def pass_on(index, source, target, begin, count, by):
+        return mesh_copy(
+            source.at[pl.ds(begin, count)],
+            target.at[pl.ds(begin, count)],
+            line_send.at[index],
+            line_recv.at[index],
+            tile_at((first + by) % RING, second, core),
+            me,
+        )
+
+    before, after, beyond = (first + 3) % RING, (first + 1) % RING, (first + 2) % RING
+    go_up, go_down = pass_on(0, mine, below, 0, held, 1), pass_on(1, mine, above, 0, held, 3)
+    on_up, on_down = pass_on(2, below, far, 0, half, 1), pass_on(3, above, far, half, half, 3)
+
+    sent = []
+
+    def deal(order, place, line):
+        reader = tile_at(place, second, core) * cut_count + me
+        owners = [pos_ref[total + reader * held + frame] >> shift for frame in range(held)]
+        for target, (by, swap) in enumerate(
+            [(2, 0), (2, 1), (1, 0), (3, 0), (1, 1), (3, 1), (0, 1), (0, 0)]
+        ):
+            target_core = core if swap == 0 else 1 - core
+            goal = tile_at(first, (second + by) % RING, target_core)
+            seen = jnp.int32(0)
+            pick = [jnp.int32(0), jnp.int32(0)]
+            for frame in range(held):
+                hit = owners[frame] == goal
+                pick[1] = jnp.where(jnp.logical_and(hit, seen == 1), frame, pick[1])
+                pick[0] = jnp.where(jnp.logical_and(hit, seen == 0), frame, pick[0])
+                seen = seen + hit.astype(jnp.int32)
+            for slot in range(2):
+                if by == 0 and swap == 0:
+                    inbox[core, second, place, slot] = line[pick[slot]]
+                else:
+                    outbox[order, target, slot] = line[pick[slot]]
+            if by or swap:
+                copy = mesh_copy(
+                    outbox.at[order, target],
+                    inbox.at[core, second, place],
+                    box_send.at[order, target],
+                    box_recv.at[core, second, place],
+                    goal,
+                    me,
+                )
+                copy.start()
+                sent.append(copy)
+
+    begin, take_left, take_right, take_across, finish = gather_steps(
+        own_ref, next_ref, rim_send, rim_recv, ring_send, ring_recv
+    )
+    begin()
+    go_up.start()
+    go_down.start()
+    deal(0, first, mine)
+    take_left()
+    take_right()
+    go_up.wait_recv()
+    on_up.start()
+    deal(1, before, below)
+    take_across()
+    go_down.wait_recv()
+    on_down.start()
+    deal(2, after, above)
+    on_up.wait_recv()
+    on_down.wait_recv()
+    deal(3, beyond, far)
+    finish()
+    for sender_core, sender_second in [(core, (second + by) % RING) for by in range(1, RING)] + [
+        (1 - core, at) for at in range(RING)
+    ]:
+        for place in range(RING):
+            mesh_copy(
+                outbox.at[0, 0],
+                inbox.at[sender_core, sender_second, place],
+                box_send.at[0, 0],
+                box_recv.at[sender_core, sender_second, place],
+                tile_at(first, second, 1 - core),
+                me,
+            ).wait_recv()
+    for copy in [go_up, go_down, on_up, on_down] + sent:
+        copy.wait_send()
+
+
+def opening(flat_positions, amplitudes, held):
+    frames_held, side, _ = amplitudes.shape
+    _, parts, height, width = held.shape
+    vmem = pl.BlockSpec(memory_space=pltpu.VMEM)
+    panel = jax.ShapeDtypeStruct((RING, parts, height, width), jnp.bfloat16)
+    own, following, inbox = pl.pallas_call(
+        opening_kernel,
         out_shape=(
-            jax.ShapeDtypeStruct((tile_count * capacity, side, side), jnp.bfloat16),
-            jax.ShapeDtypeStruct((128,), jnp.int32),
+            panel,
+            panel,
+            jax.ShapeDtypeStruct((2, RING, RING, 2, side, side), jnp.bfloat16),
         ),
-        in_specs=[
-            pl.BlockSpec(memory_space=pltpu.SMEM),
-            pl.BlockSpec(memory_space=pltpu.VMEM),
-        ],
-        out_specs=(
-            pl.BlockSpec(memory_space=pltpu.VMEM),
-            pl.BlockSpec(memory_space=pltpu.SMEM),
+        in_specs=[pl.BlockSpec(memory_space=pltpu.SMEM), vmem, vmem],
+        out_specs=(vmem, vmem, vmem),
+        scratch_shapes=[
+            *[pltpu.VMEM((frames_held, side, side), jnp.bfloat16)] * 4,
+            pltpu.VMEM((RING, 7, 2, side, side), jnp.bfloat16),
+            pltpu.SemaphoreType.DMA((4,)),
+            pltpu.SemaphoreType.DMA((4,)),
+            pltpu.SemaphoreType.DMA((RING, 7)),
+            pltpu.SemaphoreType.DMA((2, RING, RING)),
+        ]
+        + [pltpu.SemaphoreType.DMA((4,))] * 4,
+        compiler_params=pltpu.CompilerParams(
+            collective_id=1, has_side_effects=True, vmem_limit_bytes=40 << 20
         ),
-        scratch_shapes=[
-            pltpu.VMEM(amplitudes.shape, jnp.bfloat16),
-            pltpu.SMEM((tile_count * capacity,), jnp.int32),
-        ],
-        name="prep",
-    )(positions.T.reshape(-1), amplitudes)
+        name="opening",
+    )(flat_positions, amplitudes, held)
+    return own, following, inbox.reshape(-1, side, side)
+
+
+def exchange_kernel(gathers, term_ref, held_ref, new_ref, *refs):
+    own_ref, next_ref = refs[:2] if gathers else (None, None)
+    refs = refs[2:] if gathers else refs
+    out_box, in_box, far_out, far_in, near_out, near_in = refs[:6]
+    tile_send, tile_recv, cut_send, cut_recv = refs[6:10]
+    tile_count = lax.axis_size("tile")
+    tile = lax.axis_index("tile")
+    me = lax.axis_index("cuts")
+    peers = RING
+    right, left, across = (me + 1) % peers, (me + 3) % peers, (me + 2) % peers
+    has_next = tile < tile_count - 1
+    has_prev = tile > 0
+    barrier = pltpu.get_barrier_semaphore()
+    expected = greet_near(barrier)
+
+    def to_cut(source, target, sends, recvs, index, cut):
+        return mesh_copy(source, target, sends.at[index], recvs.at[index], tile, cut)
+
+    def to_tile(source, target, sends, recvs, index, by):
+        return mesh_copy(source, target, sends.at[index], recvs.at[index], tile + by, me)
+
+    def plane(half, level, part):
+        return term_ref[half, 2 * level + part]
+
+    order = [across, right, left, me]
+    forward = [
+        to_tile(out_box.at[k], in_box.at[k], tile_send, tile_recv, k, 1) for k in range(peers)
+    ]
+
+    @pl.when(has_next)
+    def _():
+        for k in range(peers):
+            for part in range(2):
+                out_box[k, part] = plane(1, order[k], part).astype(jnp.bfloat16)
+
+    @pl.when(jnp.logical_not(has_prev))
+    def _():
+        in_box[...] = jnp.zeros_like(in_box)
+
+    pl.semaphore_wait(barrier, expected)
+
+    @pl.when(has_next)
+    def _():
+        for copy in forward:
+            copy.start()
+
+    def arrived(k):
+        @pl.when(has_prev)
+        def _():
+            forward[k].wait_recv()
+
+    def joined(k, part):
+        return plane(0, order[k], part) + in_box[k, part].astype(jnp.float32)
+
+    arrived(0)
+    far_out[0] = joined(0, 0).astype(jnp.bfloat16)
+    far_out[1] = joined(0, 1).astype(jnp.bfloat16)
+    far_right = to_cut(far_out.at[0], far_in.at[0], cut_send, cut_recv, 0, right)
+    far_left = to_cut(far_out.at[1], far_in.at[1], cut_send, cut_recv, 1, left)
+    far_right.start()
+    far_left.start()
+    near_right = to_cut(near_out.at[0], near_in.at[0], cut_send, cut_recv, 2, right)
+    near_left = to_cut(near_out.at[1], near_in.at[1], cut_send, cut_recv, 3, left)
+    arrived(1)
+    near_out[0, 1] = joined(1, 1).astype(jnp.bfloat16)
+    far_right.wait_recv()
+    near_out[0, 0] = (joined(1, 0) + far_in[0].astype(jnp.float32)).astype(jnp.bfloat16)
+    near_right.start()
+    arrived(2)
+    near_out[1, 0] = joined(2, 0).astype(jnp.bfloat16)
+    far_left.wait_recv()
+    near_out[1, 1] = (joined(2, 1) + far_in[1].astype(jnp.float32)).astype(jnp.bfloat16)
+    near_left.start()
+    arrived(3)
+    for part in range(2):
+        new_ref[0, part] = joined(3, part)
+    near_right.wait_recv()
+    near_left.wait_recv()
+    for part in range(2):
+        share = (
+            new_ref[0, part]
+            + near_in[0, part].astype(jnp.float32)
+            + near_in[1, part].astype(jnp.float32)
+        )
+        fresh = held_ref[0, part] - STEP_SIZE * share
+        new_ref[0, part] = fresh
+        if gathers:
+            own_ref[me, part] = fresh.astype(jnp.bfloat16)
+
+    if gathers:
+        for step in gather_steps(own_ref, next_ref, *refs[10:]):
+            step()
+
+    for copy in (far_right, far_left, near_right, near_left):
+        copy.wait_send()
+
+    @pl.when(has_next)
+    def _():
+        for copy in forward:
+            copy.wait_send()
+
+
+def exchange(term, held, gathers, number):
+    _, parts, height, width = held.shape
+    vmem = pl.BlockSpec(memory_space=pltpu.VMEM)
+    outs = [jax.ShapeDtypeStruct(held.shape, jnp.float32)]
+    scratch = [
+        pltpu.VMEM((RING, parts, height, width), jnp.bfloat16),
+        pltpu.VMEM((RING, parts, height, width), jnp.bfloat16),
+        pltpu.VMEM((2, height, width), jnp.bfloat16),
+        pltpu.VMEM((2, height, width), jnp.bfloat16),
+        pltpu.VMEM((2, parts, height, width), jnp.bfloat16),
+        pltpu.VMEM((2, parts, height, width), jnp.bfloat16),
+    ] + [pltpu.SemaphoreType.DMA((4,))] * 4
+    if gathers:
+        outs += [jax.ShapeDtypeStruct((RING, parts, height, width), jnp.bfloat16)] * 2
+        scratch += [pltpu.SemaphoreType.DMA((4,))] * 4
+    return pl.pallas_call(
+        functools.partial(exchange_kernel, gathers),
+        out_shape=tuple(outs),
+        in_specs=[vmem] * 2,
+        out_specs=tuple([vmem] * len(outs)),
+        scratch_shapes=scratch,
+        compiler_params=pltpu.CompilerParams(
+            collective_id=number, has_side_effects=True, vmem_limit_bytes=40 << 20
+        ),
+        name="exchange",
+    )(term, held)
 
 
 def times(left, right):
@@ -249,30 +603,19 @@
     )(meta, own, following, measured, probe_field, planes)
 
 
-def passed_along(x, axis, by):
-    peers = lax.axis_size(axis)
-    pairs = [(i, i + by) for i in range(peers) if 0 <= i + by < peers]
-    return lax.ppermute(x, axis, pairs)
-
-
 def body(amplitudes, positions, probe_field, object_slices):
-    tile_count = lax.axis_size("tile")
     frames_held, side, _ = amplitudes.shape
-    capacity = max(2, 2 * frames_held // tile_count)
-    outgoing, meta = prepare(positions, amplitudes, tile_count, capacity)
-    incoming = lax.all_to_all(
-        outgoing.reshape(tile_count, capacity, side, side), "tile", split_axis=0, concat_axis=0, tiled=True
-    ).reshape(tile_count * capacity, side, side)
+    flat_positions = positions.T.reshape(-1)
+    meta = list_frames(flat_positions, frames_held, side, 2)
     planes = jnp.asarray(base_tables(side))
     current = object_slices
+    own, following, incoming = opening(flat_positions, amplitudes, current)
     for turn in range(ITERS):
-        stacked = lax.all_gather(current.astype(jnp.bfloat16), "cuts", axis=0, tiled=True)
-        following = passed_along(stacked, "tile", -1)
-        term = frame_gradient(meta, stacked, following, incoming, probe_field, planes)
-        term = term.reshape((2,) + stacked.shape)
-        moved = passed_along(term[1], "tile", 1)
-        share = lax.psum_scatter(term[0] + moved, "cuts", scatter_dimension=0, tiled=True)
-        current = current - STEP_SIZE * share
+        term = frame_gradient(meta, own, following, incoming, probe_field, planes)
+        gathers = turn < ITERS - 1
+        current, *panels = exchange(term, current, gathers, 2 + turn)
+        if gathers:
+            own, following = panels
     return current
 
 

time: 195 us -> 106 us (0.54); the launches traced: 192 us -> 105 us
  waiting for transfers between devices: 105 us -> 0 us
  Pallas kernels: 21.1 us -> 98 us
  blocking collectives: 26.5 us -> 0 us
  starting transfers between devices: 19.5 us -> 0 us
  between operations: 13.5 us -> 0.11 us
  local copies, waits for them, and re-layouts: 1.65 us -> 7.12 us
  other arithmetic: 4.99 us -> 0 us
    pallas_call x1 -> x4, Pallas kernels: 5.92 us -> 86.9 us  [the longest x2 51.2 us: exchange(): pl.pallas_call(functools.partial(exchange_kernel, gathers), out_shape=tup...]
    reduce_scatter x2 -> x0, waiting for transfers between devices: 54.2 us -> none  [body(): lax.psum_scatter(term[0] + moved, 'cuts', scatter_dimension=0, tiled=True)]
    ppermute x4 -> x0, waiting for transfers between devices: 50.6 us -> none  [passed_along(): return lax.ppermute(x, axis, pairs)]
    all_gather x2 -> x0, blocking collectives: 26.5 us -> none  [body(): lax.all_gather(current.astype(jnp.bfloat16), 'cuts', axis=0, tiled=True)]
    ppermute x4 -> x0, starting transfers between devices: 10.8 us -> none  [passed_along(): return lax.ppermute(x, axis, pairs)]
    all_to_all x1 -> x0, starting transfers between devices: 8.61 us -> none  [body(): lax.all_to_all(outgoing.reshape(tile_count, capacity, side, side), 'tile'...]
    unnamed x13 -> x20, local copies, waits for them, and re-layouts: 1.33 us -> 7.12 us
    pallas_call x2, Pallas kernels: 15.2 us -> 11.1 us  [frame_gradient(): pl.pallas_call(frames_kernel, out_shape=jax.ShapeDtypeStruct((2, 2 * slic...]
  transfers between devices with their start and end apart: 7 -> 0, of which waited for: 6 -> 0; matrix products, arithmetic and copies ran while one was open for 0% -> 0% of each run, Pallas kernels for 0% -> 0%
where the time goes in v3:
time: 106 us; the launch traced here: 105 us
  Pallas kernels  98 us (92%)
  local copies, waits for them, and re-layouts  7.12 us (7%)
    pallas_call x2, Pallas kernels, exchange(): pl.pallas_call(functools.partial(exchange_kernel, gathers), out_shape=tup...  51.2 us
    pallas_call x1, Pallas kernels, opening(): pl.pallas_call(opening_kernel, out_shape=(panel, panel, jax.ShapeDtypeStr...  33.1 us
    pallas_call x2, Pallas kernels, frame_gradient(): pl.pallas_call(frames_kernel, out_shape=jax.ShapeDtypeStruct((2, 2 * slic...  11.1 us
    unnamed x20, local copies, waits for them, and re-layouts  7.12 us
    pallas_call x1, Pallas kernels, list_frames(): pl.pallas_call(functools.partial(list_kernel, held, side.bit_length() - 1...  2.6 us

profile of v3, /device:TPU:10, one launch (start us, length us, event | category | flops | bytes accessed | tf_op | source)
XLA Modules:
  0.0 105.2 jit_solution(11461202316031085672)
XLA Ops:
  0.0 1.3 %copy.8 = s32[1,8,2,128]{3,1,2,0:T(8,128)} copy(s32[1,8,2,128]{3,2,1,0:T(2,128)} %bitcast.10) | data formatting | bytes 16384
  1.3 2.6 %listing.1.meta_ref = s32[128]{0:T(128)} custom-call(s32[2048]{0:T(1024)} %bitcast.6), custom_call_target="tpu_custom_call" | custom-call | tf_op jit(solution)/shard_map/listing/pallas_call | solution.py:68
  3.9 0.0 copy-start
  3.9 0.9 copy-done
  4.9 0.0 copy-start.2
  4.9 1.0 copy-done.2
  5.9 0.0 copy-start.3
  5.9 0.7 copy-done.3
  6.6 33.1 %opening.1 = (bf16[4,2,256,128]{3,2,1,0:T(8,128)(2,1)S(1)}, bf16[4,2,256,128]{3,2,1,0:T(8,128)(2,1)S(1)}, bf16[2,4,4,2,128,128]{5,4,3,2,1,0:T(8,128)(2,1)S(1)}) custom-call(s32[2048]{0:T(1024)S(1)} %bitcast.7, f32[8,128,128]{2,1,0:T(8,128)S(1)} %copy-done.2, f32[1,2,256,128]{3,2,1,0:T(8,128)S(1)} %copy-done), custom_call_target="tpu_custom_call" | custom-call | tf_op jit(solution)/shard_map/opening/pallas_call | solution.py:311
  39.7 0.0 copy-start.4
  39.7 0.6 copy-done.4
  40.3 0.0 copy-start.5
  40.3 0.9 copy-done.5
  41.2 0.0 copy-start.7
  41.2 0.9 copy-done.7
  42.2 0.0 copy-start.1
  42.2 5.4 %frames.2.term_ref = f32[2,8,256,128]{3,2,1,0:T(8,128)S(1)} custom-call(s32[128]{0:T(128)S(1)} %copy-done.4, bf16[4,2,256,128]{3,2,1,0:T(8,128)(2,1)S(1)} %get-tuple-element.11.own_ref, bf16[4,2,256,128]{3,2,1,0:T(8,128)(2,1)S(1)} %get-tuple-element.12.next_ref, bf16[64,128,128]{2,1,0:T(8,128)(2,1)S(1)} %bitcast.8, f32[2,128,128]{2,1,0:T(8,128)S(1)} %copy-done.5, ...), custom_call_target="tpu_custom_call" | custom-call | flops 4294967296 | bytes 6291456 | tf_op jit(solution)/shard_map/frames/pallas_call | solution.py:587
  47.6 0.0 copy-done.1
  47.6 0.0 copy-start.6
  47.6 0.0 copy-start.8
  47.6 31.4 %exchange.2 = (f32[1,2,256,128]{3,2,1,0:T(8,128)S(1)}, bf16[4,2,256,128]{3,2,1,0:T(8,128)(2,1)S(1)}, bf16[4,2,256,128]{3,2,1,0:T(8,128)(2,1)S(1)}) custom-call(f32[2,8,256,128]{3,2,1,0:T(8,128)S(1)} %frames.2.term_ref, f32[1,2,256,128]{3,2,1,0:T(8,128)S(1)} %copy-done.1), custom_call_target="tpu_custom_call" | custom-call | tf_op jit(solution)/shard_map/exchange/pallas_call | solution.py:454
  79.0 0.0 copy-done.6
  79.1 0.0 copy-done.8
  79.1 5.6 %frames.3.term_ref = f32[2,8,256,128]{3,2,1,0:T(8,128)S(1)} custom-call(s32[128]{0:T(128)S(1)} %copy-done.4, bf16[4,2,256,128]{3,2,1,0:T(8,128)(2,1)S(1)} %get-tuple-element.14.own_ref, bf16[4,2,256,128]{3,2,1,0:T(8,128)(2,1)S(1)} %get-tuple-element.15.next_ref, bf16[64,128,128]{2,1,0:T(8,128)(2,1)S(1)} %bitcast.9, f32[2,128,128]{2,1,0:T(8,128)S(1)} %copy-done.6, ...), custom_call_target="tpu_custom_call" | custom-call | flops 4294967296 | bytes 6291456 | tf_op jit(solution)/shard_map/frames/pallas_call | solution.py:587
  84.7 19.8 %exchange.3 = f32[1,2,256,128]{3,2,1,0:T(8,128)S(1)} custom-call(f32[2,8,256,128]{3,2,1,0:T(8,128)S(1)} %frames.3.term_ref, f32[1,2,256,128]{3,2,1,0:T(8,128)S(1)} %get-tuple-element.16.held_ref), custom_call_target="tpu_custom_call" | custom-call | tf_op jit(solution)/shard_map/exchange/pallas_call | solution.py:454
  104.5 0.7 copy.10
Async XLA Ops:
  3.9 1.0 copy-start
  4.9 1.0 copy-start.2
  5.9 0.7 copy-start.3
  39.7 0.6 copy-start.4
  40.3 0.9 copy-start.5
  41.2 0.9 copy-start.7
  42.2 5.5 %copy-start.1 = (f32[1,2,256,128]{3,2,1,0:T(8,128)S(1)}, f32[1,2,256,128]{3,2,1,0:T(8,128)}, u32[]{:S(2)}) copy-start(f32[1,2,256,128]{3,2,1,0:T(8,128)} %held_ref.3) | copy-start | bytes 786436
  47.6 31.4 %copy-start.6 = (f32[2,128,128]{2,1,0:T(8,128)S(1)}, f32[2,128,128]{2,1,0:T(8,128)}, u32[]{:S(2)}) copy-start(f32[2,128,128]{2,1,0:T(8,128)} %probe_ref.3) | copy-start | bytes 393220
  47.6 31.4 %copy-start.8 = (bf16[4,128,128]{2,1,0:T(8,128)(2,1)S(1)}, bf16[4,128,128]{2,1,0:T(8,128)(2,1)}, u32[]{:S(2)}) copy-start(bf16[4,128,128]{2,1,0:T(8,128)(2,1)} %constant.2.clone.planes_ref) | copy-start | bytes 393220

commit v4 on v3

--- a/solution.py
+++ b/solution.py
@@ -32,19 +32,26 @@
     return planes.astype(ml_dtypes.bfloat16)
 
 
+def row_spot(frame):
+    return frame // 128 * 256 + frame % 128
+
+
+def col_spot(frame):
+    return row_spot(frame) + 128
+
+
 def list_kernel(held, shift, capacity, pos_ref, meta_ref):
     tile_count = lax.axis_size("tile")
     cut_count = lax.axis_size("cuts")
     tile = lax.axis_index("tile")
     cut = lax.axis_index("cuts")
-    total = pos_ref.shape[0] // 2
     load = 2 * held
 
     def scan(reader, count):
-        begin = (reader * cut_count + cut) * held
+        begin = col_spot((reader * cut_count + cut) * held)
         for frame in range(held):
             meta_ref[64 + count] = reader * held + frame
-            count = count + ((pos_ref[total + begin + frame] >> shift) == tile).astype(jnp.int32)
+            count = count + ((pos_ref[begin + frame] >> shift) == tile).astype(jnp.int32)
         return count
 
     count = lax.fori_loop(0, tile_count, scan, jnp.int32(0))
@@ -56,8 +63,8 @@
         frame = reader * cut_count * held + cut * held + packed % held
         slot = jnp.where(reader == before, slot + 1, 0)
         before = reader
-        meta_ref[rank] = jnp.where(live, pos_ref[frame], 0)
-        meta_ref[32 + rank] = jnp.where(live, pos_ref[total + frame] - (tile << shift), 0)
+        meta_ref[rank] = jnp.where(live, pos_ref[row_spot(frame)], 0)
+        meta_ref[32 + rank] = jnp.where(live, pos_ref[col_spot(frame)] - (tile << shift), 0)
         core, along_z, along_x = reader % 2, reader // 2 % RING, reader // (2 * RING)
         line = jnp.where(core == 0, along_z * RING + along_x, (RING + along_x) * RING + along_z)
         meta_ref[64 + rank] = jnp.where(live, line * capacity + slot, 0)
@@ -114,85 +121,80 @@
     return 2 + has_next.astype(jnp.int32) + has_prev.astype(jnp.int32)
 
 
-def gather_steps(own_ref, next_ref, rim_send, rim_recv, ring_send, ring_recv):
-    tile_count = lax.axis_size("tile")
+class Ring:
+    def __init__(self, panel, sends, recvs):
+        tile = lax.axis_index("tile")
+        me = lax.axis_index("cuts")
+        right, left, across = (me + 1) % RING, (me + 3) % RING, (me + 2) % RING
+
+        def copy(index, level, part, cut):
+            spot = panel.at[level, part]
+            return mesh_copy(spot, spot, sends.at[index], recvs.at[index], tile, cut)
+
+        self.go_right = [copy(part, me, part, right) for part in range(2)]
+        self.go_left = [copy(2 + part, me, part, left) for part in range(2)]
+        self.from_left = [copy(part, left, part, right) for part in range(2)]
+        self.from_right = [copy(2 + part, right, part, left) for part in range(2)]
+        self.on_right, self.on_left = copy(4, left, 0, right), copy(5, right, 1, left)
+        self.far = [copy(4, across, 0, right), copy(5, across, 1, left)]
+
+    def begin(self, part):
+        self.go_right[part].start()
+        self.go_left[part].start()
+
+    def take_left(self, part):
+        self.from_left[part].wait_recv()
+        if part == 0:
+            self.on_right.start()
+
+    def take_right(self, part):
+        self.from_right[part].wait_recv()
+        if part == 1:
+            self.on_left.start()
+
+    def take_far(self, part):
+        self.far[part].wait_recv()
+
+    def settle(self):
+        for copy in self.go_right + self.go_left + [self.on_right, self.on_left]:
+            copy.wait_send()
+
+
+def rim_copies(own_ref, next_ref, sends, recvs):
     tile = lax.axis_index("tile")
     me = lax.axis_index("cuts")
-    right, left, across = (me + 1) % RING, (me + 3) % RING, (me + 2) % RING
-    has_next = tile < tile_count - 1
-    has_prev = tile > 0
-
-    def ring(index, level, part, cut):
-        spot = own_ref.at[level] if part is None else own_ref.at[level, part]
-        return mesh_copy(spot, spot, ring_send.at[index], ring_recv.at[index], tile, cut)
-
-    def rim(index, level):
-        return mesh_copy(
-            own_ref.at[level], next_ref.at[level], rim_send.at[index], rim_recv.at[index], tile - 1, me
-        )
-
-    go_right, go_left = ring(0, me, None, right), ring(1, me, None, left)
-    from_left, from_right = ring(0, left, None, right), ring(1, right, None, left)
-    on_right, on_left = ring(2, left, 0, right), ring(3, right, 1, left)
-    far_first, far_second = ring(2, across, 0, right), ring(3, across, 1, left)
-    rims = [rim(0, me), rim(1, left), rim(2, right), rim(3, across)]
-
-    def pass_rim(k):
-        @pl.when(has_prev)
-        def _():
-            rims[k].start()
-
-    def begin():
-        go_right.start()
-        go_left.start()
-        pass_rim(0)
-
-    def take_left():
-        from_left.wait_recv()
-        on_right.start()
-        pass_rim(1)
-
-    def take_right():
-        from_right.wait_recv()
-        on_left.start()
-        pass_rim(2)
-
-    def take_across():
-        far_first.wait_recv()
-        far_second.wait_recv()
-        pass_rim(3)
-
-    def finish():
-        @pl.when(has_next)
-        def _():
-            for copy in rims:
-                copy.wait_recv()
-
-        @pl.when(jnp.logical_not(has_next))
-        def _():
-            next_ref[...] = jnp.zeros_like(next_ref)
-
-        for copy in (go_right, go_left, on_right, on_left):
-            copy.wait_send()
-
-        @pl.when(has_prev)
-        def _():
-            for copy in rims:
-                copy.wait_send()
-
-    return begin, take_left, take_right, take_across, finish
+    levels = [me, (me + 3) % RING, (me + 1) % RING, (me + 2) % RING]
+    return [
+        [
+            mesh_copy(
+                own_ref.at[level, part],
+                next_ref.at[level, part],
+                sends.at[2 * role + part],
+                recvs.at[2 * role + part],
+                tile - 1,
+                me,
+            )
+            for part in range(2)
+        ]
+        for role, level in enumerate(levels)
+    ]
 
 
 def opening_kernel(
     pos_ref, amp_ref, held_ref, own_ref, next_ref, inbox, mine, below, above, far, outbox,
-    line_send, line_recv, box_send, box_recv, rim_send, rim_recv, ring_send, ring_recv,
+    amp_box, held_box, fetch, line_send, line_recv, box_send, box_recv,
+    rim_send, rim_recv, ring_send, ring_recv, next_send, next_recv,
 ):
+    fetch_held = pltpu.make_async_copy(held_ref, held_box, fetch.at[0])
+    fetch_amp = pltpu.make_async_copy(amp_ref, amp_box, fetch.at[1])
+    fetch_held.start()
+    fetch_amp.start()
     cut_count = lax.axis_size("cuts")
+    tile_count = lax.axis_size("tile")
     tile = lax.axis_index("tile")
     me = lax.axis_index("cuts")
     held, side, _ = amp_ref.shape
     shift = side.bit_length() - 1
-    total = pos_ref.shape[0] // 2
     core = tile % 2
     along_z = tile // 2 % RING
     along_x = tile // (2 * RING)
@@ -211,10 +213,12 @@
             greet(barrier, tile_at((first + by) % RING, second, target_core), me)
             greet(barrier, tile_at(first, (second + by) % RING, target_core), me)
             expected = expected + 2
+    fetch_held.wait()
     for part in range(2):
-        own_ref[me, part] = held_ref[0, part].astype(jnp.bfloat16)
+        own_ref[me, part] = held_box[0, part].astype(jnp.bfloat16)
+    fetch_amp.wait()
     for frame in range(held):
-        mine[frame] = amp_ref[frame].astype(jnp.bfloat16)
+        mine[frame] = amp_box[frame].astype(jnp.bfloat16)
     pl.semaphore_wait(barrier, expected + 1)
 
     half = held // 2
@@ -237,7 +241,7 @@
 
     def deal(order, place, line):
         reader = tile_at(place, second, core) * cut_count + me
-        owners = [pos_ref[total + reader * held + frame] >> shift for frame in range(held)]
+        owners = [pos_ref[col_spot(reader * held) + frame] >> shift for frame in range(held)]
         for target, (by, swap) in enumerate(
             [(2, 0), (2, 1), (1, 0), (3, 0), (1, 1), (3, 1), (0, 1), (0, 0)]
         ):
@@ -267,26 +271,67 @@
                 copy.start()
                 sent.append(copy)
 
-    begin, take_left, take_right, take_across, finish = gather_steps(
-        own_ref, next_ref, rim_send, rim_recv, ring_send, ring_recv
-    )
-    begin()
+    has_next = tile < tile_count - 1
+    has_prev = tile > 0
+    around = Ring(own_ref, ring_send, ring_recv)
+    beside = Ring(next_ref, next_send, next_recv)
+    rims = rim_copies(own_ref, next_ref, rim_send, rim_recv)[0]
+
+    @pl.when(has_prev)
+    def _():
+        for copy in rims:
+            copy.start()
+
     go_up.start()
     go_down.start()
+    for part in range(2):
+        around.begin(part)
     deal(0, first, mine)
-    take_left()
-    take_right()
+
+    @pl.when(has_next)
+    def _():
+        for part in range(2):
+            rims[part].wait_recv()
+            beside.begin(part)
+
+    for part in range(2):
+        around.take_left(part)
+        around.take_right(part)
     go_up.wait_recv()
     on_up.start()
     deal(1, before, below)
-    take_across()
     go_down.wait_recv()
     on_down.start()
     deal(2, after, above)
+
+    @pl.when(has_next)
+    def _():
+        for part in range(2):
+            beside.take_left(part)
+            beside.take_right(part)
+
     on_up.wait_recv()
     on_down.wait_recv()
     deal(3, beyond, far)
-    finish()
+    for part in range(2):
+        around.take_far(part)
+    around.settle()
+
+    @pl.when(has_next)
+    def _():
+        for part in range(2):
+            beside.take_far(part)
+        beside.settle()
+
+    @pl.when(jnp.logical_not(has_next))
+    def _():
+        next_ref[...] = jnp.zeros_like(next_ref)
+
+    @pl.when(has_prev)
+    def _():
+        for copy in rims:
+            copy.wait_send()
+
     for sender_core, sender_second in [(core, (second + by) % RING) for by in range(1, RING)] + [
         (1 - core, at) for at in range(RING)
     ]:
@@ -315,17 +360,20 @@
             panel,
             jax.ShapeDtypeStruct((2, RING, RING, 2, side, side), jnp.bfloat16),
         ),
-        in_specs=[pl.BlockSpec(memory_space=pltpu.SMEM), vmem, vmem],
+        in_specs=[pl.BlockSpec(memory_space=pltpu.SMEM)] + [pl.BlockSpec(memory_space=pltpu.HBM)] * 2,
         out_specs=(vmem, vmem, vmem),
         scratch_shapes=[
             *[pltpu.VMEM((frames_held, side, side), jnp.bfloat16)] * 4,
             pltpu.VMEM((RING, 7, 2, side, side), jnp.bfloat16),
+            pltpu.VMEM(amplitudes.shape, jnp.float32),
+            pltpu.VMEM(held.shape, jnp.float32),
+            pltpu.SemaphoreType.DMA((2,)),
             pltpu.SemaphoreType.DMA((4,)),
             pltpu.SemaphoreType.DMA((4,)),
             pltpu.SemaphoreType.DMA((RING, 7)),
             pltpu.SemaphoreType.DMA((2, RING, RING)),
         ]
-        + [pltpu.SemaphoreType.DMA((4,))] * 4,
+        + [pltpu.SemaphoreType.DMA((8,))] * 6,
         compiler_params=pltpu.CompilerParams(
             collective_id=1, has_side_effects=True, vmem_limit_bytes=40 << 20
         ),
@@ -359,15 +407,18 @@
         return term_ref[half, 2 * level + part]
 
     order = [across, right, left, me]
-    forward = [
-        to_tile(out_box.at[k], in_box.at[k], tile_send, tile_recv, k, 1) for k in range(peers)
-    ]
+    line_up = [(0, 0), (0, 1), (1, 1), (2, 0), (1, 0), (2, 1), (3, 0), (3, 1)]
+    forward = {
+        (k, part): to_tile(
+            out_box.at[k, part], in_box.at[k, part], tile_send, tile_recv, 2 * k + part, 1
+        )
+        for k, part in line_up
+    }
 
     @pl.when(has_next)
     def _():
-        for k in range(peers):
-            for part in range(2):
-                out_box[k, part] = plane(1, order[k], part).astype(jnp.bfloat16)
+        for k, part in line_up:
+            out_box[k, part] = plane(1, order[k], part).astype(jnp.bfloat16)
 
     @pl.when(jnp.logical_not(has_prev))
     def _():
@@ -377,42 +428,50 @@
 
     @pl.when(has_next)
     def _():
-        for copy in forward:
-            copy.start()
-
-    def arrived(k):
+        for pair in line_up:
+            forward[pair].start()
+
+    def joined(k, part):
         @pl.when(has_prev)
         def _():
-            forward[k].wait_recv()
-
-    def joined(k, part):
+            forward[k, part].wait_recv()
+
         return plane(0, order[k], part) + in_box[k, part].astype(jnp.float32)
 
-    arrived(0)
-    far_out[0] = joined(0, 0).astype(jnp.bfloat16)
-    far_out[1] = joined(0, 1).astype(jnp.bfloat16)
     far_right = to_cut(far_out.at[0], far_in.at[0], cut_send, cut_recv, 0, right)
     far_left = to_cut(far_out.at[1], far_in.at[1], cut_send, cut_recv, 1, left)
+    near_right = [
+        to_cut(near_out.at[0, part], near_in.at[0, part], cut_send, cut_recv, 2 + part, right)
+        for part in range(2)
+    ]
+    near_left = [
+        to_cut(near_out.at[1, part], near_in.at[1, part], cut_send, cut_recv, 4 + part, left)
+        for part in range(2)
+    ]
+    far_out[0] = joined(0, 0).astype(jnp.bfloat16)
     far_right.start()
+    far_out[1] = joined(0, 1).astype(jnp.bfloat16)
     far_left.start()
-    near_right = to_cut(near_out.at[0], near_in.at[0], cut_send, cut_recv, 2, right)
-    near_left = to_cut(near_out.at[1], near_in.at[1], cut_send, cut_recv, 3, left)
-    arrived(1)
     near_out[0, 1] = joined(1, 1).astype(jnp.bfloat16)
+    near_right[1].start()
+    near_out[1, 0] = joined(2, 0).astype(jnp.bfloat16)
+    near_left[0].start()
+    near_own = joined(1, 0)
     far_right.wait_recv()
-    near_out[0, 0] = (joined(1, 0) + far_in[0].astype(jnp.float32)).astype(jnp.bfloat16)
-    near_right.start()
-    arrived(2)
-    near_out[1, 0] = joined(2, 0).astype(jnp.bfloat16)
+    near_out[0, 0] = (near_own + far_in[0].astype(jnp.float32)).astype(jnp.bfloat16)
+    near_right[0].start()
+    near_own = joined(2, 1)
     far_left.wait_recv()
-    near_out[1, 1] = (joined(2, 1) + far_in[1].astype(jnp.float32)).astype(jnp.bfloat16)
-    near_left.start()
-    arrived(3)
+    near_out[1, 1] = (near_own + far_in[1].astype(jnp.float32)).astype(jnp.bfloat16)
+    near_left[1].start()
     for part in range(2):
         new_ref[0, part] = joined(3, part)
-    near_right.wait_recv()
-    near_left.wait_recv()
+    if gathers:
+        around = Ring(own_ref, *refs[12:14])
+        rims = rim_copies(own_ref, next_ref, *refs[10:12])
     for part in range(2):
+        near_right[part].wait_recv()
+        near_left[part].wait_recv()
         share = (
             new_ref[0, part]
             + near_in[0, part].astype(jnp.float32)
@@ -422,18 +481,53 @@
         new_ref[0, part] = fresh
         if gathers:
             own_ref[me, part] = fresh.astype(jnp.bfloat16)
+            around.begin(part)
+
+            @pl.when(has_prev)
+            def _():
+                rims[0][part].start()
 
     if gathers:
-        for step in gather_steps(own_ref, next_ref, *refs[10:]):
-            step()
-
-    for copy in (far_right, far_left, near_right, near_left):
+
+        def pass_rim(role, part):
+            @pl.when(has_prev)
+            def _():
+                rims[role][part].start()
+
+        for part in range(2):
+            around.take_left(part)
+            pass_rim(1, part)
+            around.take_right(part)
+            pass_rim(2, part)
+        for part in range(2):
+            around.take_far(part)
+            pass_rim(3, part)
+
+        @pl.when(has_next)
+        def _():
+            for pair in rims:
+                for copy in pair:
+                    copy.wait_recv()
+
+        @pl.when(jnp.logical_not(has_next))
+        def _():
+            next_ref[...] = jnp.zeros_like(next_ref)
+
+        around.settle()
+
+        @pl.when(has_prev)
+        def _():
+            for pair in rims:
+                for copy in pair:
+                    copy.wait_send()
+
+    for copy in [far_right, far_left] + near_right + near_left:
         copy.wait_send()
 
     @pl.when(has_next)
     def _():
-        for copy in forward:
-            copy.wait_send()
+        for pair in line_up:
+            forward[pair].wait_send()
 
 
 def exchange(term, held, gathers, number):
@@ -447,10 +541,10 @@
         pltpu.VMEM((2, height, width), jnp.bfloat16),
         pltpu.VMEM((2, parts, height, width), jnp.bfloat16),
         pltpu.VMEM((2, parts, height, width), jnp.bfloat16),
-    ] + [pltpu.SemaphoreType.DMA((4,))] * 4
+    ] + [pltpu.SemaphoreType.DMA((8,))] * 4
     if gathers:
         outs += [jax.ShapeDtypeStruct((RING, parts, height, width), jnp.bfloat16)] * 2
-        scratch += [pltpu.SemaphoreType.DMA((4,))] * 4
+        scratch += [pltpu.SemaphoreType.DMA((8,))] * 4
     return pl.pallas_call(
         functools.partial(exchange_kernel, gathers),
         out_shape=tuple(outs),
@@ -497,8 +591,13 @@
 
 
 def frames_kernel(
-    meta_ref, own_ref, next_ref, amp_ref, probe_ref, planes_ref, grad_ref, panel, tables, views, kept
+    meta_ref, own_ref, next_ref, amp_ref, probe_hbm, planes_hbm, grad_ref,
+    panel, tables, views, kept, probe_ref, planes_ref, fetch,
 ):
+    fetch_probe = pltpu.make_async_copy(probe_hbm, probe_ref, fetch.at[0])
+    fetch_planes = pltpu.make_async_copy(planes_hbm, planes_ref, fetch.at[1])
+    fetch_probe.start()
+    fetch_planes.start()
     slices = own_ref.shape[0]
     side = own_ref.shape[-1]
     for level in range(slices):
@@ -507,6 +606,8 @@
             panel[plane, 0] = own_ref[level, part].astype(jnp.float32)
             panel[plane, 1] = next_ref[level, part].astype(jnp.float32)
     grad_ref[...] = jnp.zeros_like(grad_ref)
+    fetch_probe.wait()
+    fetch_planes.wait()
     for kind in range(2):
         real, imag = planes_ref[2 * kind], planes_ref[2 * kind + 1]
         tables[2 * kind, :side, :side] = real
@@ -587,13 +688,18 @@
     return pl.pallas_call(
         frames_kernel,
         out_shape=jax.ShapeDtypeStruct((2, 2 * slices, height, side), jnp.float32),
-        in_specs=[pl.BlockSpec(memory_space=pltpu.SMEM)] + [vmem] * 5,
+        in_specs=[pl.BlockSpec(memory_space=pltpu.SMEM)]
+        + [vmem] * 3
+        + [pl.BlockSpec(memory_space=pltpu.HBM)] * 2,
         out_specs=vmem,
         scratch_shapes=[
             pltpu.VMEM((2 * slices, 2, height, side), jnp.float32),
             pltpu.VMEM((4, 2 * side, 2 * side), jnp.bfloat16),
             pltpu.VMEM((GROUP, 2 * slices, side, side), jnp.float32),
             pltpu.VMEM((GROUP, 2 * slices - 2, side, side), jnp.float32),
+            pltpu.VMEM(probe_field.shape, jnp.float32),
+            pltpu.VMEM(planes.shape, jnp.bfloat16),
+            pltpu.SemaphoreType.DMA((2,)),
         ],
         compiler_params=pltpu.CompilerParams(vmem_limit_bytes=48 << 20),
         cost_estimate=pl.CostEstimate(
@@ -605,7 +711,7 @@
 
 def body(amplitudes, positions, probe_field, object_slices):
     frames_held, side, _ = amplitudes.shape
-    flat_positions = positions.T.reshape(-1)
+    flat_positions = positions.reshape(-1, 128, 2).transpose(0, 2, 1).reshape(-1)
     meta = list_frames(flat_positions, frames_held, side, 2)
     planes = jnp.asarray(base_tables(side))
     current = object_slices

time: 106 us -> 96 us (0.906)
  the two profiles are of different devices: /device:TPU:10 before, /device:TPU:6 now
where the time goes in v4:
time: 96 us; the launch traced here: 95.7 us
  Pallas kernels  89.8 us (94%)
  local copies, waits for them, and re-layouts  5.86 us (6%)
    pallas_call x2, Pallas kernels, exchange(): pl.pallas_call(functools.partial(exchange_kernel, gathers), out_shape=tup...  47.6 us
    pallas_call x1, Pallas kernels, opening(): pl.pallas_call(opening_kernel, out_shape=(panel, panel, jax.ShapeDtypeStr...  27.8 us
    pallas_call x2, Pallas kernels, frame_gradient(): pl.pallas_call(frames_kernel, out_shape=jax.ShapeDtypeStruct((2, 2 * slic...  11.6 us
    unnamed x19, local copies, waits for them, and re-layouts  5.86 us
    pallas_call x1, Pallas kernels, list_frames(): pl.pallas_call(functools.partial(list_kernel, held, side.bit_length() - 1...  2.79 us

profile of v4, /device:TPU:6, one launch (start us, length us, event | category | flops | bytes accessed | tf_op | source)
XLA Modules:
  0.0 95.7 jit_solution(9824627575305530627)
XLA Ops:
  0.0 2.8 %listing.1.meta_ref = s32[128]{0:T(128)} custom-call(s32[2048]{0:T(1024)} %bitcast.6), custom_call_target="tpu_custom_call" | custom-call | tf_op jit(solution)/shard_map/listing/pallas_call | solution.py:75
  2.8 0.0 copy-start
  2.8 0.9 copy-done
  3.8 0.0 copy-start.2
  3.8 1.0 %copy-done.2 = f32[8,128,128]{2,1,0:T(8,128)S(1)} copy-done((f32[8,128,128]{2,1,0:T(8,128)S(1)}, f32[8,128,128]{2,1,0:T(8,128)}, u32[]{:S(2)}) %copy-start.2) | copy-done | bytes 524312
  4.8 0.0 copy-start.3
  4.8 0.7 copy-done.3
  5.5 27.8 %opening.1 = (bf16[4,2,256,128]{3,2,1,0:T(8,128)(2,1)S(1)}, bf16[4,2,256,128]{3,2,1,0:T(8,128)(2,1)S(1)}, bf16[2,4,4,2,128,128]{5,4,3,2,1,0:T(8,128)(2,1)S(1)}) custom-call(s32[2048]{0:T(1024)S(1)} %bitcast.7, f32[8,128,128]{2,1,0:T(8,128)S(1)} %copy-done.2, f32[1,2,256,128]{3,2,1,0:T(8,128)S(1)} %copy-done), custom_call_target="tpu_custom_call" | custom-call | tf_op jit(solution)/shard_map/opening/pallas_call | solution.py:356
  33.3 0.0 copy-start.4
  33.3 0.6 copy-done.4
  33.9 0.0 copy-start.5
  33.9 0.9 copy-done.5
  34.8 0.0 copy-start.7
  34.8 0.9 copy-done.7
  35.7 0.0 copy-start.1
  35.7 5.7 %frames.2.term_ref = f32[2,8,256,128]{3,2,1,0:T(8,128)S(1)} custom-call(s32[128]{0:T(128)S(1)} %copy-done.4, bf16[4,2,256,128]{3,2,1,0:T(8,128)(2,1)S(1)} %get-tuple-element.11.own_ref, bf16[4,2,256,128]{3,2,1,0:T(8,128)(2,1)S(1)} %get-tuple-element.12.next_ref, bf16[64,128,128]{2,1,0:T(8,128)(2,1)S(1)} %bitcast.8, f32[2,128,128]{2,1,0:T(8,128)S(1)} %copy-done.5, ...), custom_call_target="tpu_custom_call" | custom-call | flops 4294967296 | bytes 6291456 | tf_op jit(solution)/shard_map/frames/pallas_call | solution.py:688
  41.4 0.0 copy-done.1
  41.4 0.0 copy-start.6
  41.5 0.0 copy-start.8
  41.5 27.4 %exchange.2 = (f32[1,2,256,128]{3,2,1,0:T(8,128)S(1)}, bf16[4,2,256,128]{3,2,1,0:T(8,128)(2,1)S(1)}, bf16[4,2,256,128]{3,2,1,0:T(8,128)(2,1)S(1)}) custom-call(f32[2,8,256,128]{3,2,1,0:T(8,128)S(1)} %frames.2.term_ref, f32[1,2,256,128]{3,2,1,0:T(8,128)S(1)} %copy-done.1), custom_call_target="tpu_custom_call" | custom-call | tf_op jit(solution)/shard_map/exchange/pallas_call | solution.py:548
  68.9 0.0 copy-done.6
  68.9 0.0 copy-done.8
  68.9 5.9 %frames.3.term_ref = f32[2,8,256,128]{3,2,1,0:T(8,128)S(1)} custom-call(s32[128]{0:T(128)S(1)} %copy-done.4, bf16[4,2,256,128]{3,2,1,0:T(8,128)(2,1)S(1)} %get-tuple-element.14.own_ref, bf16[4,2,256,128]{3,2,1,0:T(8,128)(2,1)S(1)} %get-tuple-element.15.next_ref, bf16[64,128,128]{2,1,0:T(8,128)(2,1)S(1)} %bitcast.9, f32[2,128,128]{2,1,0:T(8,128)S(1)} %copy-done.6, ...), custom_call_target="tpu_custom_call" | custom-call | flops 4294967296 | bytes 6291456 | tf_op jit(solution)/shard_map/frames/pallas_call | solution.py:688
  74.8 20.2 %exchange.3 = f32[1,2,256,128]{3,2,1,0:T(8,128)S(1)} custom-call(f32[2,8,256,128]{3,2,1,0:T(8,128)S(1)} %frames.3.term_ref, f32[1,2,256,128]{3,2,1,0:T(8,128)S(1)} %get-tuple-element.16.held_ref), custom_call_target="tpu_custom_call" | custom-call | tf_op jit(solution)/shard_map/exchange/pallas_call | solution.py:548
  95.0 0.7 copy.8
Async XLA Ops:
  2.8 1.0 copy-start
  3.8 1.0 %copy-start.2 = (f32[8,128,128]{2,1,0:T(8,128)S(1)}, f32[8,128,128]{2,1,0:T(8,128)}, u32[]{:S(2)}) copy-start(f32[8,128,128]{2,1,0:T(8,128)} %amp_ref.1) | copy-start | bytes 1572868
  4.8 0.7 copy-start.3
  33.3 0.7 copy-start.4
  33.9 0.9 copy-start.5
  34.8 0.9 copy-start.7
  35.7 5.7 %copy-start.1 = (f32[1,2,256,128]{3,2,1,0:T(8,128)S(1)}, f32[1,2,256,128]{3,2,1,0:T(8,128)}, u32[]{:S(2)}) copy-start(f32[1,2,256,128]{3,2,1,0:T(8,128)} %held_ref.3) | copy-start | bytes 786436
  41.4 27.4 %copy-start.6 = (f32[2,128,128]{2,1,0:T(8,128)S(1)}, f32[2,128,128]{2,1,0:T(8,128)}, u32[]{:S(2)}) copy-start(f32[2,128,128]{2,1,0:T(8,128)} %probe_hbm.3) | copy-start | bytes 393220
  41.5 27.4 %copy-start.8 = (bf16[4,128,128]{2,1,0:T(8,128)(2,1)S(1)}, bf16[4,128,128]{2,1,0:T(8,128)(2,1)}, u32[]{:S(2)}) copy-start(bf16[4,128,128]{2,1,0:T(8,128)(2,1)} %constant.2.clone.planes_hbm) | copy-start | bytes 393220
